TPU v7x, 32 devices: a whole 2x2x4 slice. The times are simulated.
32 devices in a mesh: dp: 4 (over y, x), tm: 4 (over z), height: 2 (over core).
Axes of the slice: x: 2, y: 2, z: 4, core: 2. Of those that a mesh axis runs over, the one named last changes fastest.
Arguments:
- latents: bfloat16 [4, 8, 8, 160, 128], P('dp', 'tm', 'height'), may hold values from -40 to 40
- cotangent: bfloat16 [4, 8, 16, 320, 128], P('dp', 'tm', 'height'), may hold values from -6 to 6
- group_norm_gain: float32 [128], replicated, may hold values from 0.5 to 1.5
- group_norm_bias: float32 [128], replicated, may hold values from -3 to 3
- kernel: bfloat16 [3, 3, 384, 128], replicated, may hold values from -0.109375 to 0.109375
- kernel_bias: float32 [128], replicated, may hold values from -3 to 3
Outputs:
- upsampled: bfloat16 [4, 8, 16, 320, 128], P('dp', 'tm', 'height')
- latent_gradient: bfloat16 [4, 8, 8, 160, 128], P('dp', 'tm', 'height')
- kernel_grad: float32 [3, 3, 384, 128], replicated
- bias_grad: float32 [128], replicated
- gain_grad: float32 [128], replicated
- shift_grad: float32 [128], replicated
All inputs are finite; a program needn't handle non-finite values.
Results may differ from a plain program's by a relative error of at most 0.0051.
Values may be sent and summed in bfloat16 or wider, within the bound.
No kernel may reach another device: no remote copies, remote signals or barrier semaphores. Data moves between devices by JAX's collectives and lax.ppermute only.
A program may use at most 128 MiB of HBM per device.

v0:
```python
import jax
import jax.numpy as jnp
from jax import lax
from jax.sharding import PartitionSpec as P

GROUPS = 32


def shifted(block, axis, distance):
    devices = range(lax.axis_size(axis))
    route = [(i - distance, i) for i in devices if i - distance in devices]
    return lax.ppermute(block, axis, route)


def with_halo(block, sides, width):
    for axis, dim in sides:
        count = lax.axis_size(axis)
        forward = [(i, i + 1) for i in range(count - 1)]
        backward = [(target, source) for source, target in forward]
        low = lax.ppermute(
            lax.slice_in_dim(block, block.shape[dim] - width, None, axis=dim), axis, forward
        )
        high = lax.ppermute(lax.slice_in_dim(block, 0, width, axis=dim), axis, backward)
        block = jnp.concatenate([low, block, high], axis=dim)
    return block


def conv(padded, kernel, out_t, out_r, out_w):
    total = jnp.zeros((out_t * out_r * out_w, kernel.shape[-1]), jnp.float32)
    for i in range(3):
        for j in range(3):
            slab = jnp.concatenate(
                [padded[i : i + out_t, j : j + out_r, k : k + out_w] for k in range(3)], axis=-1
            )
            total = total + jnp.dot(
                slab.reshape(-1, slab.shape[-1]), kernel[i, j], preferred_element_type=jnp.float32
            )
    return total.reshape(out_t, out_r, out_w, kernel.shape[-1])


def tap_terms(padded, flat_grad, index, out_t, out_r, out_w):
    row_list = []
    for j in range(3):
        slab = jnp.concatenate(
            [padded[index : index + out_t, j : j + out_r, k : k + out_w] for k in range(3)], axis=-1
        )
        row_list.append(
            lax.dot_general(
                slab.reshape(-1, slab.shape[-1]),
                flat_grad,
                (((0,), (0,)), ((), ())),
                preferred_element_type=jnp.float32,
            )
        )
    return jnp.stack(row_list)


def flip_kernel(kernel):
    channel_total = kernel.shape[-1]
    split = kernel.reshape(3, 3, 3, channel_total, channel_total)[::-1, ::-1, ::-1]
    return jnp.swapaxes(split, 3, 4).reshape(3, 3, 3 * channel_total, channel_total)


def local(latents, cotangent, group_norm_gain, group_norm_bias, kernel, kernel_bias):
    frame_total, row_total, width_total, channel_total = latents.shape[1:]
    group_size = channel_total // GROUPS
    count = (
        frame_total
        * lax.axis_size("tm")
        * row_total
        * lax.axis_size("height")
        * width_total
        * group_size
    )
    grouped = (
        latents[0]
        .astype(jnp.float32)
        .reshape(frame_total, row_total, width_total, GROUPS, group_size)
    )
    first_sum, square_sum = lax.psum(
        (jnp.sum(grouped, axis=(0, 1, 2, 4)), jnp.sum(grouped * grouped, axis=(0, 1, 2, 4))),
        ("tm", "height"),
    )
    group_mean = first_sum / count
    var = square_sum / count - group_mean * group_mean
    centred_input = grouped - group_mean[:, None]
    inverse_deviation = lax.rsqrt(var + 1e-06)
    normalized_times_gradient = centred_input * inverse_deviation[:, None]
    normalized_input = normalized_times_gradient.reshape(
        frame_total, row_total, width_total, channel_total
    )
    preactivation = normalized_input * group_norm_gain + group_norm_bias
    sig = jax.nn.sigmoid(preactivation)
    act = (preactivation * sig).astype(jnp.bfloat16)
    first = lax.axis_index("tm") == 0
    top = lax.axis_index("height") == 0
    bottom = lax.axis_index("height") == lax.axis_size("height") - 1
    past = shifted(act, "tm", 1)
    past = jnp.where(first, jnp.broadcast_to(act[:1], past.shape), past)
    timed = jnp.concatenate([past, act], axis=0)
    tall = with_halo(timed, (("height", 1),), 1)
    upper = jnp.where(top, tall[:, 1:2], tall[:, :1])
    lower = jnp.where(bottom, tall[:, -2:-1], tall[:, -1:])
    tall = jnp.concatenate([upper, tall[:, 1:-1], lower], axis=1)
    padded = jnp.pad(tall, ((0, 0), (0, 0), (1, 1), (0, 0)), mode="edge")
    conv_out = (conv(padded, kernel, frame_total, row_total, width_total) + kernel_bias).astype(
        jnp.bfloat16
    )
    upsampled = jnp.broadcast_to(
        conv_out[:, :, None, :, None, :], (frame_total, row_total, 2, width_total, 2, channel_total)
    ).reshape(frame_total, 2 * row_total, 2 * width_total, channel_total)
    dconv32 = jnp.sum(
        cotangent[0].reshape(frame_total, row_total, 2, width_total, 2, channel_total),
        axis=(2, 4),
        dtype=jnp.float32,
    )
    bias_part = jnp.sum(dconv32, axis=(0, 1, 2))
    dconv = dconv32.astype(jnp.bfloat16)
    flat_grad = dconv.reshape(-1, channel_total)
    kernel_part = jnp.stack(
        [
            tap_terms(padded, flat_grad, index, frame_total, row_total, width_total)
            for index in range(3)
        ]
    )
    ahead = shifted(dconv, "tm", -1)
    extended = jnp.concatenate([dconv, ahead], axis=0)
    tall_grad = with_halo(extended, (("height", 1),), 1)
    wide = jnp.pad(tall_grad, ((2, 0), (1, 1), (2, 2), (0, 0)))
    dpadded = conv(wide, flip_kernel(kernel), frame_total + 2, row_total + 2, width_total + 2)
    folded_w = dpadded[:, :, 1:-1]
    folded_w = folded_w.at[:, :, 0].add(dpadded[:, :, 0])
    folded_w = folded_w.at[:, :, -1].add(dpadded[:, :, -1])
    folded_h = folded_w[:, 1:-1]
    folded_h = folded_h.at[:, 0].add(jnp.where(top, folded_w[:, 0], 0.0))
    folded_h = folded_h.at[:, -1].add(jnp.where(bottom, folded_w[:, -1], 0.0))
    dact = folded_h[2:]
    dact = dact.at[0].add(jnp.where(first, folded_h[0] + folded_h[1], 0.0))
    preact_gradient = dact * sig * (1.0 + preactivation * (1.0 - sig))
    gain_partial = jnp.sum(preact_gradient * normalized_input, axis=(0, 1, 2))
    shift_part = jnp.sum(preact_gradient, axis=(0, 1, 2))
    normalized_gradient = (preact_gradient * group_norm_gain).reshape(
        frame_total, row_total, width_total, GROUPS, group_size
    )
    sum_a, sum_b = lax.psum(
        (
            jnp.sum(normalized_gradient, axis=(0, 1, 2, 4)),
            jnp.sum(normalized_gradient * normalized_times_gradient, axis=(0, 1, 2, 4)),
        ),
        ("tm", "height"),
    )
    first_mean = sum_a / count
    second_mean = sum_b / count
    latent_gradient = (
        (
            inverse_deviation[:, None]
            * (
                normalized_gradient
                - first_mean[:, None]
                - normalized_times_gradient * second_mean[:, None]
            )
        )
        .reshape(frame_total, row_total, width_total, channel_total)
        .astype(jnp.bfloat16)
    )
    kernel_grad, bias_grad, gain_grad, shift_grad = lax.psum(
        (kernel_part, bias_part, gain_partial, shift_part), ("dp", "tm", "height")
    )
    return (upsampled[None], latent_gradient[None], kernel_grad, bias_grad, gain_grad, shift_grad)


def solution(mesh):
    return jax.shard_map(
        local,
        mesh=mesh,
        in_specs=(
            P("dp", "tm", "height", None, None),
            P("dp", "tm", "height", None, None),
            P(),
            P(),
            P(),
            P(),
        ),
        out_specs=(
            P("dp", "tm", "height", None, None),
            P("dp", "tm", "height", None, None),
            P(),
            P(),
            P(),
            P(),
        ),
        check_vma=False,
    )
```

profile of v0, /device:TPU:0, one launch (start us, length us, event | category | flops | bytes accessed | tf_op | source)
XLA Modules:
  0.0 362.2 jit_solution(9138160146500872676)
XLA Ops:
  7.2 3.6 reduce_sum.109
  10.8 1.3 collective-permute-start.3
  12.1 1.2 convert_reduce_fusion.1
  13.7 19.6 %all-reduce.3 = (f32[32]{0:T(128)S(1)}, f32[32]{0:T(128)S(1)}) all-reduce(f32[32]{0:T(128)S(1)} %reduce_sum.108, f32[32]{0:T(128)S(1)} %reduce_sum.105), channel_id=1, replica_groups=mesh['dp'=4,'tm'=4,'height'=2] {'tm','height'}, use_global_device_ids=true, to_apply=%region_5.6 | all-reduce | flops 64 | bytes 512 | tf_op jit(solution)/shard_map/psum | solution.py:80
  33.8 1.7 copy.12
  36.4 1.3 collective-permute-start.5
  37.7 3.2 collective-permute-start.4
  41.8 3.6 %fusion.11 = bf16[6,8,164,128]{3,2,1,0:T(8,128)(2,1)S(1)} fusion(bf16[4,1,160,128]{3,2,1,0:T(8,128)(2,1)S(1)} %collective-permute-done.5, bf16[4,1,160,128]{3,2,1,0:T(8,128)(2,1)S(1)} %collective-permute-done.4, bf16[2,4,160,128]{3,2,1,0:T(8,128)(2,1)} %collective-permute-done.3, bf16[2,4,160,128]{3,2,1,0:T(8,128)(2,1)S(1)} %reduce_sum.109), kind=kLoop, calls=%fused_computation.42 | loop fusion | flops 29220864 | bytes 2998272 | tf_op jit(solution)/shard_map/concatenate | solution.py:24
  45.4 2.5 fusion.89
  47.9 7.5 %fusion.88 = (bf16[4,6,162,128]{3,2,1,0:T(8,128)(2,1)}, bf16[4,6,162,128]{3,2,1,0:T(8,128)(2,1)}, bf16[4,6,162,128]{3,2,1,0:T(8,128)(2,1)}, bf16[4,6,162,128]{3,...) fusion(bf16[6,8,164,128]{3,2,1,0:T(8,128)(2,1)S(1)} %fusion.11), kind=kLoop, calls=%fused_computation.182 | loop fusion | bytes 37822464 | tf_op jit(solution)/shard_map/slice | solution.py:33
  55.4 2.1 pad_maximum_fusion
  57.5 2.5 reshape.300
  60.0 3.0 reshape.303
  63.0 4.8 %pad_maximum_fusion.2 = (bf16[4,6,162,384]{3,2,1,0:T(8,128)(2,1)}, bf16[4,6,162,384]{3,2,1,0:T(8,128)(2,1)}) fusion(bf16[4,6,162,128]{3,2,1,0:T(8,128)(2,1)} %get-tuple-element.99, bf16[4,6,162,128]{3,2,1,0:T(8,128)(2,1)} %get-tuple-element.100, bf16[4,6,162,128]{3,2,1,0:T(8,128)(2,1)} %get-tuple-element.102, ...), kind=kLoop, calls=%fused_computation.23 | loop fusion | flops 17915904 | bytes 11943936 | tf_op jit(solution)/shard_map/concatenate | solution.py:32
  67.8 4.7 %reshape.304 = bf16[3888,384]{1,0:T(8,128)(2,1)} reshape(bf16[4,6,162,384]{3,2,1,0:T(8,128)(2,1)} %get-tuple-element.147) | data formatting | bytes 5971968 | tf_op jit(solution)/shard_map/reshape | solution.py:36
  72.5 4.8 %pad_maximum_fusion.3 = (bf16[4,6,162,384]{3,2,1,0:T(8,128)(2,1)}, bf16[4,6,162,384]{3,2,1,0:T(8,128)(2,1)}) fusion(bf16[4,6,162,128]{3,2,1,0:T(8,128)(2,1)} %get-tuple-element.96, bf16[4,6,162,128]{3,2,1,0:T(8,128)(2,1)} %get-tuple-element.97, bf16[4,6,162,128]{3,2,1,0:T(8,128)(2,1)} %get-tuple-element.98, bf16[4,6,162,128]{3,2,1,0:T(8,128)(2,1)} %get-tuple-element.93, ...), kind=kLoop, calls=%fused_computation.24 | loop fusion | flops 17915904 | bytes 11943936 | tf_op jit(solution)/shard_map/concatenate | solution.py:32
  77.3 4.7 %reshape.305 = bf16[3888,384]{1,0:T(8,128)(2,1)} reshape(bf16[4,6,162,384]{3,2,1,0:T(8,128)(2,1)} %get-tuple-element.149) | data formatting | bytes 5971968 | tf_op jit(solution)/shard_map/reshape | solution.py:36
  82.0 4.8 %reshape.306 = bf16[3888,384]{1,0:T(8,128)(2,1)} reshape(bf16[4,6,162,384]{3,2,1,0:T(8,128)(2,1)} %get-tuple-element.150) | data formatting | bytes 5971968 | tf_op jit(solution)/shard_map/reshape | solution.py:36
  86.7 4.8 %pad_maximum_fusion.5 = (bf16[4,6,162,384]{3,2,1,0:T(8,128)(2,1)}, bf16[4,6,162,384]{3,2,1,0:T(8,128)(2,1)}) fusion(bf16[4,6,162,128]{3,2,1,0:T(8,128)(2,1)} %get-tuple-element.90, bf16[4,6,162,128]{3,2,1,0:T(8,128)(2,1)} %get-tuple-element.91, bf16[4,6,162,128]{3,2,1,0:T(8,128)(2,1)} %get-tuple-element.92, bf16[4,6,162,128]{3,2,1,0:T(8,128)(2,1)} %get-tuple-element.87, ...), kind=kLoop, calls=%fused_computation.26 | loop fusion | flops 17915904 | bytes 11943936 | tf_op jit(solution)/shard_map/concatenate | solution.py:32
  91.5 4.7 %reshape.307 = bf16[3888,384]{1,0:T(8,128)(2,1)} reshape(bf16[4,6,162,384]{3,2,1,0:T(8,128)(2,1)} %get-tuple-element.151) | data formatting | bytes 5971968 | tf_op jit(solution)/shard_map/reshape | solution.py:36
  96.2 4.6 %reshape.308 = bf16[3888,384]{1,0:T(8,128)(2,1)} reshape(bf16[4,6,162,384]{3,2,1,0:T(8,128)(2,1)} %get-tuple-element.152) | data formatting | bytes 5971968 | tf_op jit(solution)/shard_map/reshape | solution.py:36
  100.9 3.9 %pad_maximum_fusion.7 = bf16[4,6,162,384]{3,2,1,0:T(8,128)(2,1)} fusion(bf16[4,6,162,128]{3,2,1,0:T(8,128)(2,1)} %get-tuple-element.84, bf16[4,6,162,128]{3,2,1,0:T(8,128)(2,1)} %get-tuple-element.85, bf16[4,6,162,128]{3,2,1,0:T(8,128)(2,1)} %get-tuple-element.86), kind=kLoop, calls=%fused_computation.28 | loop fusion | flops 8957952 | bytes 5971968 | tf_op jit(solution)/shard_map/concatenate | solution.py:32
  104.7 4.7 %reshape.309 = bf16[3888,384]{1,0:T(8,128)(2,1)} reshape(bf16[4,6,162,384]{3,2,1,0:T(8,128)(2,1)} %pad_maximum_fusion.7) | data formatting | bytes 5971968 | tf_op jit(solution)/shard_map/reshape | solution.py:36
  109.4 4.8 %reshape.310 = bf16[3888,384]{1,0:T(8,128)(2,1)} reshape(bf16[4,6,162,384]{3,2,1,0:T(8,128)(2,1)} %get-tuple-element.148) | data formatting | bytes 5971968 | tf_op jit(solution)/shard_map/reshape | solution.py:36
  114.3 3.1 fusion.67
  117.4 1.2 convolution_add_fusion.7
  119.2 1.2 convolution_add_fusion.6
  121.1 1.3 convolution_add_fusion.5
  122.9 1.2 convolution_add_fusion.4
  124.8 1.3 convolution_add_fusion.3
  126.6 1.2 convolution_add_fusion.2
  128.5 1.3 convolution_add_fusion.1
  130.3 1.2 convolution_add_fusion
  131.5 1.5 reshape.311
  133.0 1.8 slice.617
  138.5 1.6 collective-permute-start
  140.5 18.3 %all-reduce.2 = (f32[32]{0:T(128)S(1)}, f32[32]{0:T(128)S(1)}) all-reduce(f32[32]{0:T(128)S(1)} %reduce_sum.115, f32[32]{0:T(128)S(1)} %reduce_sum.112), channel_id=1, replica_groups=mesh['dp'=4,'tm'=4,'height'=2] {'tm','height'}, use_global_device_ids=true, to_apply=%region_12.13 | all-reduce | flops 64 | bytes 512 | tf_op jit(solution)/shard_map/psum | solution.py:145
  159.1 1.3 collective-permute-start.1
  160.6 37.9 %all-reduce.1 = (f32[128]{0:T(128)}, f32[128]{0:T(128)}, f32[128]{0:T(128)}) all-reduce(f32[128]{0:T(128)S(1)} %convert_reduce_fusion, f32[128]{0:T(128)S(1)} %get-tuple-element.66, f32[128]{0:T(128)S(1)} %get-tuple-element.69), channel_id=1, replica_groups=mesh['dp'=4,'tm'=4,'height'=2] {'dp','tm','height'}, use_global_device_ids=true, to_apply=%region_15.16 | all-reduce | flops 384 | bytes 3072 | tf_op jit(solution)/shard_map/psum | solution.py:166
  198.5 1.3 collective-permute-start.2
  208.5 1.5 convolution_bitcast_fusion.8
  210.1 1.3 fusion.76
  212.3 1.6 pad_maximum_fusion.23
  215.1 1.3 pad_maximum_fusion.9
  216.5 1.8 convolution_add_fusion.15
  222.5 127.4 %all-reduce.6.cloned.1.call-done = f32[3,3,384,128]{3,2,1,0:T(8,128)} async-done(((f32[3,3,384,128]{3,2,1,0:T(8,128)}), f32[3,3,384,128]{3,2,1,0:T(8,128)}) %all-reduce.6.cloned.1.call-update) | async-done | bytes 1769488 | tf_op jit(solution)/shard_map/psum | solution.py:166
  349.9 2.2 broadcast_in_dim.30
  352.1 2.8 copy.28
  (135 shorter events, 26.0 us)
Async XLA Ops:
  7.2 26.5 %copy-start.14 = (bf16[3,3,384,128]{3,2,1,0:T(8,128)(2,1)S(1)}, bf16[3,3,384,128]{3,2,1,0:T(8,128)(2,1)}, u32[]{:S(2)}) copy-start(bf16[3,3,384,128]{3,2,1,0:T(8,128)(2,1)} %param.20) | copy-start | bytes 2654212
  7.2 342.8 %all-reduce.6.cloned.1.call-start = ((), (), s32[]{:S(2)}) async-start(), calls=%async_computation | async-start | bytes 3538944 | tf_op jit(solution)/shard_map/psum | solution.py:166
  10.8 197.1 %copy-start.16 = (bf16[2,4,160,128]{3,2,1,0:T(8,128)(2,1)}, bf16[2,4,160,128]{3,2,1,0:T(8,128)(2,1)S(1)}, u32[]{:S(2)}) copy-start(bf16[2,4,160,128]{3,2,1,0:T(8,128)(2,1)S(1)} %reduce_sum.109) | copy-start | bytes 983044
  10.8 24.7 %collective-permute-start.3 = (bf16[2,4,160,128]{3,2,1,0:T(8,128)(2,1)S(1)}, bf16[2,4,160,128]{3,2,1,0:T(8,128)(2,1)}, u32[]{:S(2)}, u32[]{:S(2)}) collective-permute-start(bf16[2,4,160,128]{3,2,1,0:T(8,128)(2,1)S(1)} %reduce_sum.109), channel_id=1, source_target_pairs={{2,0},{4,2},{6,4},{3,1},{5,3},{7,5},{10,8},{12,10},{14,12},{11,9},... | collective-permute-start | bytes 983048 | tf_op jit(solution)/shard_map/ppermute | solution.py:12
  33.7 7.2 %copy-start.7 = (bf16[1,2,8,320,128]{4,3,2,1,0:T(8,128)(2,1)S(1)}, bf16[1,2,8,320,128]{4,3,2,1,0:T(8,128)(2,1)}, u32[]{:S(2)}) copy-start(bf16[1,2,8,320,128]{4,3,2,1,0:T(8,128)(2,1)} %param.17) | copy-start | bytes 3932164
  36.4 5.2 %collective-permute-start.5 = (bf16[4,1,160,128]{3,2,1,0:T(8,128)(2,1)S(1)}, bf16[4,1,160,128]{3,2,1,0:T(8,128)(2,1)S(1)}, u32[]{:S(2)}, u32[]{:S(2)}) collective-permute-start(bf16[4,1,160,128]{3,2,1,0:T(8,128)(2,1)S(1)} %get-tuple-element.136), channel_id=1, source_target_pairs={{1,0},{3,2},{5,4},{7,6},{9,8},{11,10},{13,12},{15,14},{17,16},{19,... | collective-permute-start | bytes 491528 | tf_op jit(solution)/shard_map/ppermute | solution.py:23
  37.7 4.1 %collective-permute-start.4 = (bf16[4,1,160,128]{3,2,1,0:T(8,128)(2,1)S(1)}, bf16[4,1,160,128]{3,2,1,0:T(8,128)(2,1)S(1)}, u32[]{:S(2)}, u32[]{:S(2)}) collective-permute-start(bf16[4,1,160,128]{3,2,1,0:T(8,128)(2,1)S(1)} %get-tuple-element.135), channel_id=1, source_target_pairs={{0,1},{2,3},{4,5},{6,7},{8,9},{10,11},{12,13},{14,15},{16,17},{18,... | collective-permute-start | bytes 491528 | tf_op jit(solution)/shard_map/ppermute | solution.py:20
  114.3 3.1 copy-start.13
  117.4 1.8 copy-start
  119.2 1.8 copy-start.1
  121.1 1.8 copy-start.2
  122.9 1.8 copy-start.3
  124.8 1.8 copy-start.4
  126.6 1.8 copy-start.6
  128.5 1.8 copy-start.5
  137.0 1.0 copy-start.18
  137.0 1.0 copy-start.26
  137.0 1.0 copy-start.28
  138.5 20.6 %collective-permute-start = (bf16[2,4,160,128]{3,2,1,0:T(8,128)(2,1)S(1)}, bf16[2,4,160,128]{3,2,1,0:T(8,128)(2,1)S(1)}, u32[]{:S(2)}, u32[]{:S(2)}) collective-permute-start(bf16[2,4,160,128]{3,2,1,0:T(8,128)(2,1)S(1)} %get-tuple-element.139), channel_id=1, source_target_pairs={{0,2},{2,4},{4,6},{1,3},{3,5},{5,7},{8,10},{10,12},{12,14},{9,11},... | collective-permute-start | bytes 983048 | tf_op jit(solution)/shard_map/ppermute | solution.py:12
  159.1 39.4 %collective-permute-start.1 = (bf16[4,1,160,128]{3,2,1,0:T(8,128)(2,1)S(1)}, bf16[4,1,160,128]{3,2,1,0:T(8,128)(2,1)S(1)}, u32[]{:S(2)}, u32[]{:S(2)}) collective-permute-start(bf16[4,1,160,128]{3,2,1,0:T(8,128)(2,1)S(1)} %pad_maximum_fusion.28), channel_id=1, source_target_pairs={{0,1},{2,3},{4,5},{6,7},{8,9},{10,11},{12,13},{14,15},{16,17},{18,... | collective-permute-start | bytes 491528 | tf_op jit(solution)/shard_map/ppermute | solution.py:20
  198.5 3.3 collective-permute-start.2
  203.4 11.0 %copy-start.20 = (bf16[2,4,160,128]{3,2,1,0:T(8,128)(2,1)}, bf16[2,4,160,128]{3,2,1,0:T(8,128)(2,1)S(1)}, u32[]{:S(2)}) copy-start(bf16[2,4,160,128]{3,2,1,0:T(8,128)(2,1)S(1)} %get-tuple-element.118) | copy-start | bytes 983044
  203.9 10.5 %copy-start.22 = (bf16[2,4,160,128]{3,2,1,0:T(8,128)(2,1)}, bf16[2,4,160,128]{3,2,1,0:T(8,128)(2,1)S(1)}, u32[]{:S(2)}) copy-start(bf16[2,4,160,128]{3,2,1,0:T(8,128)(2,1)S(1)} %get-tuple-element.109) | copy-start | bytes 983044
  204.6 9.8 %copy-start.24 = (bf16[2,4,160,128]{3,2,1,0:T(8,128)(2,1)}, bf16[2,4,160,128]{3,2,1,0:T(8,128)(2,1)S(1)}, u32[]{:S(2)}) copy-start(bf16[2,4,160,128]{3,2,1,0:T(8,128)(2,1)S(1)} %get-tuple-element.129) | copy-start | bytes 983044
  208.5 1.6 copy-start.15
  208.5 2.8 copy-start.17
  213.9 1.0 copy-start.11
  215.0 1.4 copy-start.19
  216.4 1.8 copy-start.10
  216.4 2.2 copy-start.8
  218.2 1.2 copy-start.12
  219.9 1.0 copy-start.21
  219.9 1.1 copy-start.23
  219.9 1.2 copy-start.25
  220.3 1.3 copy-start.9
  221.6 0.9 copy-start.27
Sparse Core Ops, SparseCore 0:
  216.5 133.3 all-reduce.5
where the time goes:
time: 367 us; the launch traced here: 362 us
  waiting for transfers between devices  129 us (35%)
  blocking collectives  75.8 us (21%)
  local copies, waits for them, and re-layouts  66.7 us (18%)
  other arithmetic  41.4 us (11%)
  matrix products  24.4 us (7%)
  between operations  15.3 us (4%)
  starting transfers between devices  9.99 us (3%)
    psum x1, waiting for transfers between devices, local(): lax.psum((kernel_part, bias_part, gain_partial, shift_part), ('dp', 'tm',...  127 us
    reshape x9, local copies, waits for them, and re-layouts, conv(): slab.reshape(-1, slab.shape[-1])  38.4 us
    psum x1, blocking collectives, local(): lax.psum((kernel_part, bias_part, gain_partial, shift_part), ('dp', 'tm',...  37.9 us
    concatenate x12, other arithmetic, conv(): jnp.concatenate([padded[i:i + out_t, j:j + out_r, k:k + out_w] for k in r...  24.7 us
    psum x1, blocking collectives, local(): lax.psum((jnp.sum(grouped, axis=(0, 1, 2, 4)), jnp.sum(grouped * grouped,...  19.6 us
    dot_general x18, matrix products, conv(): jnp.dot(slab.reshape(-1, slab.shape[-1]), kernel[i, j], preferred_element...  19.1 us
    psum x1, blocking collectives, local(): lax.psum((jnp.sum(normalized_gradient, axis=(0, 1, 2, 4)), jnp.sum(normal...  18.3 us
    slice x6, local copies, waits for them, and re-layouts, conv(): padded[i:i + out_t, j:j + out_r, k:k + out_w]  11 us
  transfers between devices with their start and end apart: 7, of which 3 were waited for; matrix products, arithmetic and copies ran while one was open for 3% of the time, Pallas kernels for 0%

commit v1 on v0

v1 whole, which is shorter than its diff:
```python
import functools

import jax
import jax.numpy as jnp
from jax import lax
from jax.experimental import pallas as pl
from jax.experimental.pallas import tpu as pltpu
from jax.sharding import PartitionSpec as P

GROUPS = 32
F32 = jnp.float32
BF16 = jnp.bfloat16
TAB = 32
VMEM = pl.BlockSpec(memory_space=pltpu.VMEM)


def call(body, outs, *args, scratch=(), flops=1_000_000):
    moved = sum(a.size * a.dtype.itemsize for a in (*args, *outs))
    return pl.pallas_call(
        body,
        out_shape=tuple(outs),
        in_specs=[VMEM] * len(args),
        out_specs=tuple([VMEM] * len(outs)),
        scratch_shapes=list(scratch),
        cost_estimate=pl.CostEstimate(flops=flops, bytes_accessed=moved, transcendentals=0),
    )(*args)


def shape(dims, dtype):
    return jax.ShapeDtypeStruct(dims, dtype)


def swap(block, axis, distance):
    count = lax.axis_size(axis)
    return lax.ppermute(block, axis, [(i, i ^ distance) for i in range(count)])


def moved(block, frames, rows):
    n_t, n_h = lax.axis_size("tm"), lax.axis_size("height")
    route = []
    for t in range(n_t):
        for h in range(n_h):
            if 0 <= t + frames < n_t and 0 <= h + rows < n_h:
                route.append(((t + frames) * n_h + h + rows, t * n_h + h))
    return lax.ppermute(block, ("tm", "height"), route)


def across(block, frames):
    n_t = lax.axis_size("tm")
    route = []
    for t in range(n_t):
        for h in range(2):
            if 0 <= t + frames < n_t:
                route.append(((t + frames) * 2 + 1 - h, t * 2 + h))
    return lax.ppermute(block, ("tm", "height"), route)


def facing(edges, frames):
    if len(edges) == 1:
        other = across(edges[0], frames)
        return [other]
    return [moved(edges[0], frames, -1), moved(edges[1], frames, 1)]


def tree(values):
    while len(values) > 1:
        values = [values[i] + values[i + 1] for i in range(0, len(values), 2)]
    return values[0]


def group_sum(x):
    lane = lax.broadcasted_iota(jnp.int32, x.shape, 1)
    n = x.shape[1]
    x = x + jnp.where(lane % 2 == 0, pltpu.roll(x, n - 1, 1), pltpu.roll(x, 1, 1))
    return x + jnp.where(lane % 4 < 2, pltpu.roll(x, n - 2, 1), pltpu.roll(x, 2, 1))


def packed(table):
    high = table.astype(BF16).astype(F32)
    rest = table - high
    mid = rest.astype(BF16).astype(F32)
    low = (rest - mid).astype(BF16).astype(F32)
    return jnp.concatenate([high, mid, low, jnp.zeros_like(low)], axis=0).astype(BF16)


def unpacked(rows):
    rows = rows.astype(F32)
    return (rows[0:8] + rows[8:16]) + rows[16:24]


def before(x, edge):
    row = lax.broadcasted_iota(jnp.int32, x.shape, 0)
    return jnp.where(row == 0, x if edge else 0.0, pltpu.roll(x, 1, 0))


def after(x, edge):
    row = lax.broadcasted_iota(jnp.int32, x.shape, 0)
    return jnp.where(row == x.shape[0] - 1, x if edge else 0.0, pltpu.roll(x, x.shape[0] - 1, 0))


def stats_body(lat_ref, out_ref):
    t_n, r_n, w_n, c_n = lat_ref.shape
    total = jnp.zeros((8, c_n), F32)
    for t in range(t_n):
        for r in range(r_n):
            total += jnp.sum(lat_ref[t, r].astype(F32).reshape(w_n // 8, 8, c_n), axis=0)
    mean = jnp.sum(total, axis=0, keepdims=True) / (t_n * r_n * w_n)
    square = jnp.zeros((8, c_n), F32)
    for t in range(t_n):
        for r in range(r_n):
            x = (lat_ref[t, r].astype(F32) - mean).reshape(w_n // 8, 8, c_n)
            square += jnp.sum(x * x, axis=0)
    square = jnp.sum(square, axis=0, keepdims=True)
    row = lax.broadcasted_iota(jnp.int32, (8, c_n), 0)
    out_ref[...] = jnp.where(row == 0, mean, jnp.where(row == 1, square, 0.0))


def fold_body(edge_n, cot_ref, out_ref, bias_ref, *rest):
    edge_refs, wide = rest[:edge_n], rest[edge_n]
    t_n, r2, w2, c_n = cot_ref.shape
    r_n, w_n = r2 // 2, w2 // 2
    total = jnp.zeros((8, c_n), F32)
    for t in range(t_n):
        for r in range(r_n):
            slot = (t * r_n + r) % 2
            wide[slot] = cot_ref[t, 2 * r].astype(F32) + cot_ref[t, 2 * r + 1].astype(F32)
            value = wide[slot, pl.ds(0, w_n, stride=2), :] + wide[slot, pl.ds(1, w_n, stride=2), :]
            total += jnp.sum(value.reshape(w_n // 8, 8, c_n), axis=0)
            out_ref[t, r] = value.astype(BF16)
    bias_ref[...] = jnp.broadcast_to(jnp.sum(total, axis=0, keepdims=True), (8, c_n))
    edges(out_ref, edge_refs, r_n)


def edges(ref, edge_refs, r_n):
    if len(edge_refs) == 1:
        row = jnp.where(lax.axis_index("height") == 0, r_n - 1, 0)
        edge_refs[0][...] = ref[:, row]
    else:
        edge_refs[0][...] = ref[:, r_n - 1]
        edge_refs[1][...] = ref[:, 0]


def main_body(
    n_edge, cells, n_h,
    lat_ref, mine_ref, other_ref, grad_ref, halo_ref, kernel_ref, gain_ref, shift_ref, bias_ref, *rest,
):
    edge_refs, corner_refs, rest = rest[:n_edge], rest[n_edge : 2 * n_edge], rest[2 * n_edge :]
    keep_ref, table_ref, dpre_ref, norm_ref = rest[:4]
    send_refs, (acts, fold, weight, slope, hats, sums) = rest[4 : 3 + n_h], rest[3 + n_h :]
    t_n, r_n, w_n, c_n = lat_ref.shape
    h = lax.axis_index("height")
    top = (h == 0).astype(F32)
    bottom = (h == n_h - 1).astype(F32)
    first = (lax.axis_index("tm") == 0).astype(F32)

    a, b = mine_ref[...], other_ref[...]
    gap = a[0:1] - b[0:1]
    channel_mean = (a[0:1] + b[0:1]) * 0.5
    square = a[1:2] + b[1:2] + gap * gap * (cells / 4)
    channel_mean = jnp.broadcast_to(channel_mean, (8, c_n))
    size = c_n // GROUPS
    mean = group_sum(channel_mean) * (1.0 / size)
    off = channel_mean - mean
    var = group_sum(jnp.broadcast_to(square, (8, c_n)) + off * off * cells) * (1.0 / (cells * size))
    rstd = lax.rsqrt(var + 1e-06)
    row = lax.broadcasted_iota(jnp.int32, (8, c_n), 0)
    norm_ref[...] = jnp.where(row == 0, mean, rstd)
    mean, rstd = mean[0:1], rstd[0:1]
    gain, shift = gain_ref[...], shift_ref[...]

    for t in range(t_n):
        for r in range(r_n):
            at = pl.ds((t * r_n + r) * w_n, w_n)
            hat = (lat_ref[t, r].astype(F32) - mean) * rstd
            pre = hat * gain + shift
            sig = jax.nn.sigmoid(pre)
            act = pre * sig
            hats[at, :] = hat
            slope[at, :] = sig * (1.0 + pre * (1.0 - sig))
            acts[at, 0:c_n] = before(act, True).astype(BF16)
            acts[at, c_n : 2 * c_n] = act.astype(BF16)
            acts[at, 2 * c_n :] = after(act, True).astype(BF16)

    def source(f, r):
        if 0 <= r < r_n:
            return (grad_ref[f, r] if f < t_n else halo_ref[f - t_n, r]).astype(F32)
        refs = edge_refs if f < t_n else corner_refs
        ref = refs[0] if r < 0 else refs[-1]
        return ref[f % t_n].astype(F32) * ((1.0 - top) if r < 0 else (1.0 - bottom))

    for j in range(3):
        for r in range(r_n):
            frame = []
            for f in range(t_n + 2):
                value = source(f, r + 1 - j)
                if j == 0 and r == 0:
                    value = value + source(f, 0) * top
                if j == 2 and r == r_n - 1:
                    value = value + source(f, r_n - 1) * bottom
                frame.append(value)
            for i in range(3):
                lanes = pl.ds((i * 3 + j) * c_n, c_n)
                for t in range(t_n):
                    value = frame[t + 2 - i]
                    if t == 0 and i < 2:
                        value = value + first * (frame[0] + frame[1] if i == 0 else frame[0])
                    fold[pl.ds((t * r_n + r) * w_n, w_n), lanes] = value.astype(BF16)

    product = lax.dot_general(
        acts[...], fold[...], (((0,), (0,)), ((), ())), preferred_element_type=F32
    )
    for ij in range(9):
        sums[pl.ds(ij * 3 * c_n, 3 * c_n), :] = product[:, ij * c_n : (ij + 1) * c_n]
    share = keep_ref.shape[0]
    if sums.shape[0] > 27 * c_n:
        sums[27 * c_n :, :] = jnp.zeros((sums.shape[0] - 27 * c_n, c_n), F32)
    keep_ref[...] = sums[pl.ds(h * share, share), :]
    for s, ref in enumerate(send_refs, 1):
        ref[0:share] = sums[pl.ds((h ^ s) * share, share), :].astype(BF16)

    for ij in range(9):
        weight[:, ij * c_n : (ij + 1) * c_n] = kernel_ref[ij // 3, ij % 3]
    total_a = jnp.zeros((8, c_n), F32)
    total_b = jnp.zeros((8, c_n), F32)
    for t in range(t_n):
        back = lax.dot_general(
            fold[pl.ds(t * r_n * w_n, r_n * w_n), :], weight[...], (((1,), (1,)), ((), ())),
            preferred_element_type=F32,
        )
        for r in range(r_n):
            slab = back[r * w_n : (r + 1) * w_n]
            low, mid, high = (slab[:, k * c_n : (k + 1) * c_n] for k in range(3))
            col = lax.broadcasted_iota(jnp.int32, low.shape, 0)
            dact = (
                mid + after(low, False) + before(high, False)
                + jnp.where(col == 0, low, 0.0) + jnp.where(col == w_n - 1, high, 0.0)
            )
            at = pl.ds((t * r_n + r) * w_n, w_n)
            dpre = dact * slope[at, :]
            dpre_ref[t, r] = dpre
            total_a += jnp.sum((dpre * hats[at, :]).reshape(w_n // 8, 8, c_n), axis=0)
            total_b += jnp.sum(dpre.reshape(w_n // 8, 8, c_n), axis=0)
    total_a = jnp.sum(total_a, axis=0, keepdims=True)
    total_b = jnp.sum(total_b, axis=0, keepdims=True)
    table = jnp.where(row == 0, bias_ref[...], jnp.where(row == 1, total_a, jnp.where(row == 2, total_b, 0.0)))
    table_ref[...] = table
    for ref in send_refs:
        ref[share:] = packed(table)


def first_sum_body(n_h, n_dp, keep_ref, table_ref, *rest):
    got, (own_ref, out_table), sends = rest[: n_h - 1], rest[n_h - 1 : n_h + 1], rest[n_h + 1 : -1]
    total = rest[-1]
    share, piece = keep_ref.shape[0], own_ref.shape[0]
    value = keep_ref[...]
    for ref in got:
        value = value + ref[0:share].astype(F32)
    total[...] = value
    table = tree([unpacked(packed(table_ref[...]))] + [unpacked(ref[share:]) for ref in got])
    out_table[...] = table
    me = lax.axis_index("dp")
    own_ref[...] = total[pl.ds(me * piece, piece), :]
    for s, ref in enumerate(sends, 1):
        ref[0:piece] = total[pl.ds((me ^ s) * piece, piece), :].astype(BF16)
        ref[piece:] = packed(table)


def second_sum_body(own_ref, table_ref, *rest):
    got, out_ref = rest[:-1], rest[-1]
    piece = own_ref.shape[0]
    value = own_ref[...]
    for ref in got:
        value = value + ref[0:piece].astype(F32)
    out_ref[0:piece] = value.astype(BF16)
    own = unpacked(packed(table_ref[...]))
    table = tree([own] + [unpacked(ref[piece:]) for ref in got])
    row = lax.broadcasted_iota(jnp.int32, table.shape, 0)
    kept = jnp.where(row == 0, table, jnp.where(row < 3, own, pltpu.roll(table, 2, 0)))
    out_ref[piece:] = packed(kept)


def pair_sum_body(a_ref, b_ref, out_ref):
    piece = a_ref.shape[0] - TAB
    out_ref[0:piece] = (a_ref[0:piece].astype(F32) + b_ref[0:piece].astype(F32)).astype(BF16)
    out_ref[piece:] = packed(unpacked(a_ref[piece:]) + unpacked(b_ref[piece:]))


def last_sum_body(a_ref, b_ref, out_ref, table_ref):
    piece = out_ref.shape[0]
    out_ref[...] = (a_ref[0:piece].astype(F32) + b_ref[0:piece].astype(F32)).astype(BF16)
    table_ref[...] = unpacked(a_ref[piece:]) + unpacked(b_ref[piece:])


def gather_body(own_ref, *rest):
    got, out_ref = rest[:-1], rest[-1]
    piece = own_ref.shape[0]
    me = lax.axis_index("dp")
    for s, ref in enumerate((own_ref, *got)):
        out_ref[pl.ds((me ^ s) * piece, piece), :] = ref[...]


def spread_body(own_ref, *rest):
    got, out_ref = rest[:-1], rest[-1]
    share, rows = own_ref.shape[0], out_ref.shape[0]
    h = lax.axis_index("height")
    for s, ref in enumerate((own_ref, *got)):
        for q in range(1 + len(got)):

            def put(ref=ref, q=q):
                count = min(share, rows - q * share)
                out_ref[q * share : q * share + count] = ref[0:count].astype(F32)

            pl.when((h ^ s) == q)(put)


def forward_body(
    n_edge, n_h,
    lat_ref, past_ref, norm_ref, kernel_ref, gain_ref, shift_ref, offset_ref, *rest,
):
    edge_refs, corner_refs, rest = rest[:n_edge], rest[n_edge : 2 * n_edge], rest[2 * n_edge :]
    out_ref, acts, slabs, weight, wide = rest
    t_n, r_n, w_n, c_n = lat_ref.shape
    h = lax.axis_index("height")
    mean, rstd = norm_ref[0:1], norm_ref[1:2]
    gain, shift = gain_ref[...], shift_ref[...]

    def silu(x):
        pre = (x.astype(F32) - mean) * rstd * gain + shift
        return (pre * jax.nn.sigmoid(pre)).astype(BF16)

    def act_of(f, r):
        if 0 <= r < r_n:
            return silu(past_ref[f, r] if f < 2 else lat_ref[f - 2, r])
        refs = corner_refs if f < 2 else edge_refs
        return silu((refs[0] if r < 0 else refs[-1])[f % 2])

    for f in range(t_n + 2):
        for r in range(-1, r_n + 1):
            acts[f, r + 1] = act_of(f, r)

    @pl.when(lax.axis_index("tm") == 0)
    def _():
        for f in range(2):
            for r in range(r_n + 2):
                acts[f, r] = acts[2, r]

    @pl.when(h == 0)
    def _():
        for f in range(t_n + 2):
            acts[f, 0] = acts[f, 1]

    @pl.when(h == n_h - 1)
    def _():
        for f in range(t_n + 2):
            acts[f, r_n + 1] = acts[f, r_n]

    for ij in range(9):
        i, j = ij // 3, ij % 3
        for k in range(3):
            weight[ij * c_n : (ij + 1) * c_n, k * c_n : (k + 1) * c_n] = kernel_ref[i, j, k * c_n : (k + 1) * c_n, :]
        for t in range(t_n):
            for r in range(r_n):
                slabs[(t * r_n + r) * w_n : (t * r_n + r + 1) * w_n, ij * c_n : (ij + 1) * c_n] = acts[t + i, r + j]
    offset = offset_ref[...]
    for t in range(t_n):
        value = jnp.dot(slabs[pl.ds(t * r_n * w_n, r_n * w_n), :], weight[...], preferred_element_type=F32)
        for r in range(r_n):
            slab = value[r * w_n : (r + 1) * w_n]
            low, mid, high = (slab[:, k * c_n : (k + 1) * c_n] for k in range(3))
            conv = before(low, True) + mid + after(high, True) + offset
            slot = r % 2
            conv = conv.astype(BF16).astype(F32)
            wide[slot, pl.ds(0, w_n, stride=2), :] = conv
            wide[slot, pl.ds(1, w_n, stride=2), :] = conv
            both = wide[slot].astype(BF16)
            out_ref[t, 2 * r] = both
            out_ref[t, 2 * r + 1] = both


def last_body(cells, dpre_ref, lat_ref, norm_ref, table_ref, gain_ref, out_ref, bias_ref, gains_ref, shifts_ref):
    t_n, r_n, w_n, c_n = lat_ref.shape
    table, gain = table_ref[...], gain_ref[...]
    mean, rstd = norm_ref[0:1], norm_ref[1:2]
    scale = 1.0 / (cells * (c_n // GROUPS))
    means = group_sum(table * gain) * scale
    mean_b, mean_a = means[1:2], means[2:3]
    bias_ref[...] = table[0:1]
    gains_ref[...] = table[3:4]
    shifts_ref[...] = table[4:5]
    for t in range(t_n):
        for r in range(r_n):
            hat = (lat_ref[t, r].astype(F32) - mean) * rstd
            out_ref[t, r] = (rstd * (dpre_ref[t, r] * gain - mean_a - hat * mean_b)).astype(BF16)


def local(latents, cotangent, group_norm_gain, group_norm_bias, kernel, kernel_bias):
    lat, cot = latents[0], cotangent[0]
    t_n, r_n, w_n, c_n = lat.shape
    n_dp, n_t, n_h = (lax.axis_size(axis) for axis in ("dp", "tm", "height"))
    n_edge = 1 if n_h == 2 else 2
    gain, shift, offset = (v.reshape(1, c_n) for v in (group_norm_gain, group_norm_bias, kernel_bias))
    grid = (t_n, r_n, w_n, c_n)
    edge = (t_n, w_n, c_n)
    rows = 27 * c_n
    unit = n_h * n_dp * 16
    total = -(-rows // unit) * unit
    share, piece = total // n_h, total // (n_h * n_dp)

    grad, bias_part, *edge_list = call(
        functools.partial(fold_body, n_edge),
        [shape(grid, BF16), shape((8, c_n), F32)] + [shape(edge, BF16)] * n_edge,
        cot,
        scratch=[pltpu.VMEM((2, 2 * w_n, c_n), F32)],
    )
    (stats,) = call(stats_body, [shape((8, c_n), F32)], lat)
    halo = moved(grad, 1, 0)
    edge_rows = facing(edge_list, 0)
    corner_rows = facing(edge_list, 1)

    rounds = [("height", 1 << i) for i in range(n_h.bit_length() - 1)]
    rounds += [("tm", 1 << i) for i in range(n_t.bit_length() - 1)]
    cells = t_n * r_n * w_n
    other = None
    for axis, distance in rounds:
        if other is not None:
            gap = stats[0:1] - other[0:1]
            stats = jnp.concatenate(
                [
                    (stats[0:1] + other[0:1]) * 0.5,
                    stats[1:2] + other[1:2] + gap * gap * (cells / 4),
                    jnp.zeros((6, c_n), F32),
                ]
            )
        other = swap(stats, axis, distance)
        cells = cells * 2

    keep, table, dpre, norm, *sends = call(
        functools.partial(main_body, n_edge, cells, n_h),
        [shape((share, c_n), F32), shape((8, c_n), F32), shape(grid, F32), shape((8, c_n), F32)]
        + [shape((share + TAB, c_n), BF16)] * (n_h - 1),
        lat, stats, other, grad, halo, kernel, gain, shift, bias_part, *edge_rows, *corner_rows,
        scratch=[
            pltpu.VMEM((t_n * r_n * w_n, 3 * c_n), BF16),
            pltpu.VMEM((t_n * r_n * w_n, 9 * c_n), BF16),
            pltpu.VMEM((3 * c_n, 9 * c_n), BF16),
            pltpu.VMEM((t_n * r_n * w_n, c_n), F32),
            pltpu.VMEM((t_n * r_n * w_n, c_n), F32),
            pltpu.VMEM((total, c_n), F32),
        ],
        flops=4 * 27 * t_n * r_n * w_n * c_n * c_n,
    )

    past = moved(lat, -1, 0)
    if n_edge == 1:
        row = jnp.where(lax.axis_index("height") == 0, r_n - 1, 0)
        lat_edges = [lax.dynamic_index_in_dim(lat, row, 1, keepdims=False)]
    else:
        lat_edges = [lat[:, r_n - 1], lat[:, 0]]
    lat_rows = facing(lat_edges, 0)
    lat_corners = facing(lat_edges, -1)

    got = [swap(send, "height", s) for s, send in enumerate(sends, 1)]
    own, table, *sends = call(
        functools.partial(first_sum_body, n_h, n_dp),
        [shape((piece, c_n), F32), shape((8, c_n), F32)] + [shape((piece + TAB, c_n), BF16)] * (n_dp - 1),
        keep, table, *got,
        scratch=[pltpu.VMEM((share, c_n), F32)],
    )
    got = [swap(send, "dp", s) for s, send in enumerate(sends, 1)]
    (part,) = call(second_sum_body, [shape((piece + TAB, c_n), BF16)], own, table, *got)
    distance = 1
    while distance < n_t:
        other = swap(part, "tm", distance)
        distance *= 2
        if distance < n_t:
            (part,) = call(pair_sum_body, [shape((piece + TAB, c_n), BF16)], part, other)
    part, table = call(last_sum_body, [shape((piece, c_n), BF16), shape((8, c_n), F32)], part, other)
    got = [swap(part, "dp", s) for s in range(1, n_dp)]
    (half,) = call(gather_body, [shape((share, c_n), BF16)], part, *got)
    got = [swap(half, "height", s) for s in range(1, n_h)]
    (kernel_grad,) = call(spread_body, [shape((rows, c_n), F32)], half, *got)

    (upsampled,) = call(
        functools.partial(forward_body, n_edge, n_h),
        [shape(cot.shape, BF16)],
        lat, past, norm, kernel, gain, shift, offset, *lat_rows, *lat_corners,
        scratch=[
            pltpu.VMEM((t_n + 2, r_n + 2, w_n, c_n), BF16),
            pltpu.VMEM((t_n * r_n * w_n, 9 * c_n), BF16),
            pltpu.VMEM((9 * c_n, 3 * c_n), BF16),
            pltpu.VMEM((2, 2 * w_n, c_n), F32),
        ],
        flops=2 * 27 * t_n * r_n * w_n * c_n * c_n,
    )
    latent_gradient, bias_grad, gain_grad, shift_grad = call(
        functools.partial(last_body, cells),
        [shape(grid, BF16)] + [shape((1, c_n), F32)] * 3,
        dpre, lat, norm, table, gain,
    )
    return (
        upsampled[None],
        latent_gradient[None],
        kernel_grad.reshape(kernel.shape),
        bias_grad.reshape(c_n),
        gain_grad.reshape(c_n),
        shift_grad.reshape(c_n),
    )


def solution(mesh):
    split = P("dp", "tm", "height", None, None)
    return jax.shard_map(
        local,
        mesh=mesh,
        in_specs=(split, split, P(), P(), P(), P()),
        out_specs=(split, split, P(), P(), P(), P()),
        check_vma=False,
    )
```

time: 367 us -> 100 us (0.27); the launches traced: 362 us -> 99.8 us
  waiting for transfers between devices: 129 us -> 37.1 us
  blocking collectives: 75.8 us -> 0 us
  local copies, waits for them, and re-layouts: 66.7 us -> 5.75 us
  other arithmetic: 41.4 us -> 0.92 us
  Pallas kernels: 0 us -> 29.7 us
  matrix products: 24.4 us -> 0 us
  starting transfers between devices: 9.99 us -> 25.5 us
  between operations: 15.3 us -> 0.79 us
    psum x1 -> x0, waiting for transfers between devices: 127 us -> none  [local(): lax.psum((kernel_part, bias_part, gain_partial, shift_part), ('dp', 'tm',...]
    psum x3 -> x0, blocking collectives: 75.8 us -> none  [the longest x1 37.9 us: local(): lax.psum((kernel_part, bias_part, gain_partial, shift_part), ('dp', 'tm',...]
    reshape x10 -> x0, local copies, waits for them, and re-layouts: 39.9 us -> none  [the longest x9 38.4 us: conv(): slab.reshape(-1, slab.shape[-1])]
    ppermute x6 -> x19, waiting for transfers between devices: 1.2 us -> 37.1 us  [the longest x13 30.2 us: swap(): return lax.ppermute(block, axis, [(i, i ^ distance) for i in range(count)])]
    pallas_call x0 -> x11, Pallas kernels: none -> 29.7 us  [call(): pl.pallas_call(body, out_shape=tuple(outs), in_specs=[VMEM] * len(args),...]
    concatenate x15 -> x2, other arithmetic: 29.4 us -> 0.14 us  [local(): jnp.concatenate([(stats[0:1] + other[0:1]) * 0.5, stats[1:2] + other[1:2]...]
    dot_general x27 -> x0, matrix products: 24.4 us -> none  [the longest x18 19.1 us: conv(): jnp.dot(slab.reshape(-1, slab.shape[-1]), kernel[i, j], preferred_element...]
    ppermute x6 -> x19, starting transfers between devices: 9.95 us -> 25.5 us  [the longest x13 18.2 us: swap(): return lax.ppermute(block, axis, [(i, i ^ distance) for i in range(count)])]
  transfers between devices with their start and end apart: 7 -> 19, of which waited for: 3 -> 11; matrix products, arithmetic and copies ran while one was open for 3% -> 0% of each run, Pallas kernels for 0% -> 10%
where the time goes in v1:
time: 100 us; the launch traced here: 99.8 us
  waiting for transfers between devices  37.1 us (37%)
  Pallas kernels  29.7 us (30%)
  starting transfers between devices  25.5 us (26%)
  local copies, waits for them, and re-layouts  5.75 us (6%)
    ppermute x13, waiting for transfers between devices, swap(): return lax.ppermute(block, axis, [(i, i ^ distance) for i in range(count)])  30.2 us
    pallas_call x11, Pallas kernels, call(): pl.pallas_call(body, out_shape=tuple(outs), in_specs=[VMEM] * len(args),...  29.7 us
    ppermute x13, starting transfers between devices, swap(): return lax.ppermute(block, axis, [(i, i ^ distance) for i in range(count)])  18.2 us
    ppermute x4, waiting for transfers between devices, across(): return lax.ppermute(block, ('tm', 'height'), route)  6.88 us
    unnamed x38, local copies, waits for them, and re-layouts  5.66 us
    ppermute x4, starting transfers between devices, across(): return lax.ppermute(block, ('tm', 'height'), route)  3.71 us
    ppermute x2, starting transfers between devices, moved(): return lax.ppermute(block, ('tm', 'height'), route)  3.57 us
  transfers between devices with their start and end apart: 19, of which 11 were waited for; matrix products, arithmetic and copies ran while one was open for 0% of the time, Pallas kernels for 10%

profile of v1, /device:TPU:0, one launch (start us, length us, event | category | flops | bytes accessed | tf_op | source)
XLA Modules:
  0.0 99.8 jit_solution(8731311762703218015)
XLA Ops:
  0.6 1.7 %shard_map.109 = f32[8,128]{1,0:T(8,128)} custom-call(bf16[2,4,160,128]{3,2,1,0:T(8,128)(2,1)} %bitcast.14), custom_call_target="tpu_custom_call" | custom-call | flops 1000000 | bytes 331776 | tf_op jit(solution)/shard_map/pallas_call | solution.py:19
  2.4 0.5 collective-permute-start.1
  2.9 1.0 collective-permute-done.1
  3.9 0.8 multiply_add_fusion.1
  4.7 2.9 %collective-permute-start.2 = (f32[8,128]{1,0:T(8,128)S(1)}, f32[8,128]{1,0:T(8,128)S(1)}, u32[]{:S(2)}, u32[]{:S(2)}) collective-permute-start(f32[8,128]{1,0:T(8,128)S(1)} %maximum_maximum_fusion), channel_id=1, source_target_pairs={{0,2},{2,0},{4,6},{6,4},{1,3},{3,1},{5,7},{7,5},{8,10},{10,8},{12,... | collective-permute-start | bytes 12296 | tf_op jit(solution)/shard_map/ppermute | solution.py:35
  7.6 2.3 %shard_map.110 = (bf16[2,4,160,128]{3,2,1,0:T(8,128)(2,1)}, f32[8,128]{1,0:T(8,128)}, bf16[2,160,128]{2,1,0:T(8,128)(2,1)}) custom-call(bf16[2,8,320,128]{3,2,1,0:T(8,128)(2,1)} %bitcast.19), custom_call_target="tpu_custom_call" | custom-call | flops 1000000 | bytes 1724416 | tf_op jit(solution)/shard_map/pallas_call | solution.py:19
  10.0 1.3 %collective-permute-start.6 = (bf16[2,160,128]{2,1,0:T(8,128)(2,1)}, bf16[2,160,128]{2,1,0:T(8,128)(2,1)S(1)}, u32[]{:S(2)}, u32[]{:S(2)}) collective-permute-start(bf16[2,160,128]{2,1,0:T(8,128)(2,1)} %get-tuple-element.27), channel_id=1, source_target_pairs={{3,0},{2,1},{5,2},{4,3},{7,4},{6,5},{11,8},{10,9},{13,10},{12,11},... | collective-permute-start | bytes 245768 | tf_op jit(solution)/shard_map/ppermute | solution.py:55
  11.2 1.3 %collective-permute-start.4 = (bf16[2,4,160,128]{3,2,1,0:T(8,128)(2,1)}, bf16[2,4,160,128]{3,2,1,0:T(8,128)(2,1)S(1)}, u32[]{:S(2)}, u32[]{:S(2)}) collective-permute-start(bf16[2,4,160,128]{3,2,1,0:T(8,128)(2,1)} %get-tuple-element.25.grad_ref), channel_id=1, source_target_pairs={{2,0},{3,1},{4,2},{5,3},{6,4},{7,5},{10,8},{11,9},{12,10},{13,11},... | collective-permute-start | bytes 983048 | tf_op jit(solution)/shard_map/ppermute | solution.py:45
  12.6 4.8 %collective-permute-start.3 = (f32[8,128]{1,0:T(8,128)S(1)}, f32[8,128]{1,0:T(8,128)S(1)}, u32[]{:S(2)}, u32[]{:S(2)}) collective-permute-start(f32[8,128]{1,0:T(8,128)S(1)} %maximum_maximum_fusion.1.mine_ref), channel_id=1, source_target_pairs={{0,4},{2,6},{4,0},{6,2},{1,5},{3,7},{5,1},{7,3},{8,12},{10,14},{12... | collective-permute-start | bytes 12296 | tf_op jit(solution)/shard_map/ppermute | solution.py:35
  17.5 7.8 %collective-permute-done.3.other_ref = f32[8,128]{1,0:T(8,128)S(1)} collective-permute-done((f32[8,128]{1,0:T(8,128)S(1)}, f32[8,128]{1,0:T(8,128)S(1)}, u32[]{:S(2)}, u32[]{:S(2)}) %collective-permute-start.3) | collective-permute-done | bytes 4128 | tf_op jit(solution)/shard_map/ppermute | solution.py:35
  25.3 0.5 copy-done.18
  25.9 0.1 copy-done.12
  26.1 6.8 %shard_map.111 = (f32[1728,128]{1,0:T(8,128)}, f32[8,128]{1,0:T(8,128)}, f32[2,4,160,128]{3,2,1,0:T(8,128)}, f32[8,128]{1,0:T(8,128)}, bf16[1760,128]{1,0:T(8,128)(2,1)}) custom-call(bf16[2,4,160,128]{3,2,1,0:T(8,128)(2,1)} %bitcast.15, f32[8,128]{1,0:T(8,128)} %copy-done.11, f32[8,128]{1,0:T(8,128)} %copy-done.18, ...), custom_call_target="tpu_custom_call" | custom-call | flops 2264924160 | bytes 4043776 | tf_op jit(solution)/shard_map/pallas_call | solution.py:19
  32.8 2.0 %collective-permute-done.9.rest_0_ = bf16[1760,128]{1,0:T(8,128)(2,1)S(1)} collective-permute-done((bf16[1760,128]{1,0:T(8,128)(2,1)}, bf16[1760,128]{1,0:T(8,128)(2,1)S(1)}, u32[]{:S(2)}, u32[]{:S(2)}) %collective-permute-start.9) | collective-permute-done | bytes 450592 | tf_op jit(solution)/shard_map/ppermute | solution.py:35
  34.8 0.8 copy-done.1
  35.6 2.2 %shard_map.113 = (f32[432,128]{1,0:T(8,128)}, f32[8,128]{1,0:T(8,128)}, bf16[464,128]{1,0:T(8,128)(2,1)}, bf16[464,128]{1,0:T(8,128)(2,1)}, bf16[464,128]{1,0:T(8,128)(2,1)}) custom-call(f32[1728,128]{1,0:T(8,128)} %get-tuple-element.30.keep_ref, f32[8,128]{1,0:T(8,128)} %get-tuple-element.31.table_ref, bf16[1760,128]{1,0:T(8,128)(2,1)} %copy-done.1), custom_call_target="tpu_custom_call" | custom-call | flops 1000000 | bytes 1921024 | tf_op jit(solution)/shard_map/pallas_call | solution.py:19
  37.8 1.5 %collective-permute-start.10 = (bf16[464,128]{1,0:T(8,128)(2,1)}, bf16[464,128]{1,0:T(8,128)(2,1)S(1)}, u32[]{:S(2)}, u32[]{:S(2)}) collective-permute-start(bf16[464,128]{1,0:T(8,128)(2,1)} %get-tuple-element.35), channel_id=1, source_target_pairs={{0,8},{8,0},{16,24},{24,16},{1,9},{9,1},{17,25},{25,17},{2,10},{10... | collective-permute-start | bytes 356360 | tf_op jit(solution)/shard_map/ppermute | solution.py:35
  39.3 1.5 %collective-permute-start.11 = (bf16[464,128]{1,0:T(8,128)(2,1)}, bf16[464,128]{1,0:T(8,128)(2,1)S(1)}, u32[]{:S(2)}, u32[]{:S(2)}) collective-permute-start(bf16[464,128]{1,0:T(8,128)(2,1)} %get-tuple-element.36), channel_id=1, source_target_pairs={{0,16},{8,24},{16,0},{24,8},{1,17},{9,25},{17,1},{25,9},{2,18},{10... | collective-permute-start | bytes 356360 | tf_op jit(solution)/shard_map/ppermute | solution.py:35
  40.8 0.5 collective-permute-start.12
  41.3 2.1 %collective-permute-done.10.rest_0_ = bf16[464,128]{1,0:T(8,128)(2,1)S(1)} collective-permute-done((bf16[464,128]{1,0:T(8,128)(2,1)}, bf16[464,128]{1,0:T(8,128)(2,1)S(1)}, u32[]{:S(2)}, u32[]{:S(2)}) %collective-permute-start.10) | collective-permute-done | bytes 118816 | tf_op jit(solution)/shard_map/ppermute | solution.py:35
  43.4 3.6 %collective-permute-done.11.rest_1_ = bf16[464,128]{1,0:T(8,128)(2,1)S(1)} collective-permute-done((bf16[464,128]{1,0:T(8,128)(2,1)}, bf16[464,128]{1,0:T(8,128)(2,1)S(1)}, u32[]{:S(2)}, u32[]{:S(2)}) %collective-permute-start.11) | collective-permute-done | bytes 118816 | tf_op jit(solution)/shard_map/ppermute | solution.py:35
  47.1 0.6 copy-done.6
  47.7 1.8 %shard_map.114.a_ref = bf16[464,128]{1,0:T(8,128)(2,1)} custom-call(f32[432,128]{1,0:T(8,128)} %get-tuple-element.33.own_ref, f32[8,128]{1,0:T(8,128)} %get-tuple-element.34.table_ref, bf16[464,128]{1,0:T(8,128)(2,1)} %copy-done.5, bf16[464,128]{1,0:T(8,128)(2,1)} %copy-done.6, bf16[464,128]{1,0:T(8,128)(2,1)} %copy-done.7), custom_call_target="tpu_custom_call" | custom-call | flops 1000000 | bytes 700416 | tf_op jit(solution)/shard_map/pallas_call | solution.py:19
  49.6 1.5 %collective-permute-start.13 = (bf16[464,128]{1,0:T(8,128)(2,1)}, bf16[464,128]{1,0:T(8,128)(2,1)S(1)}, u32[]{:S(2)}, u32[]{:S(2)}) collective-permute-start(bf16[464,128]{1,0:T(8,128)(2,1)} %shard_map.114.a_ref), channel_id=1, source_target_pairs={{0,2},{2,0},{4,6},{6,4},{1,3},{3,1},{5,7},{7,5},{8,10},{10,8},{12,... | collective-permute-start | bytes 356360 | tf_op jit(solution)/shard_map/ppermute | solution.py:35
  51.1 3.5 %collective-permute-done.13.b_ref = bf16[464,128]{1,0:T(8,128)(2,1)S(1)} collective-permute-done((bf16[464,128]{1,0:T(8,128)(2,1)}, bf16[464,128]{1,0:T(8,128)(2,1)S(1)}, u32[]{:S(2)}, u32[]{:S(2)}) %collective-permute-start.13) | collective-permute-done | bytes 118816 | tf_op jit(solution)/shard_map/ppermute | solution.py:35
  54.6 0.6 copy-done.3
  55.3 1.6 %shard_map.115.a_ref = bf16[464,128]{1,0:T(8,128)(2,1)} custom-call(bf16[464,128]{1,0:T(8,128)(2,1)} %shard_map.114.a_ref, bf16[464,128]{1,0:T(8,128)(2,1)} %copy-done.3), custom_call_target="tpu_custom_call" | custom-call | flops 1000000 | bytes 356352 | tf_op jit(solution)/shard_map/pallas_call | solution.py:19
  56.9 1.4 %collective-permute-start.14 = (bf16[464,128]{1,0:T(8,128)(2,1)}, bf16[464,128]{1,0:T(8,128)(2,1)S(1)}, u32[]{:S(2)}, u32[]{:S(2)}) collective-permute-start(bf16[464,128]{1,0:T(8,128)(2,1)} %shard_map.115.a_ref), channel_id=1, source_target_pairs={{0,4},{2,6},{4,0},{6,2},{1,5},{3,7},{5,1},{7,3},{8,12},{10,14},{12... | collective-permute-start | bytes 356360 | tf_op jit(solution)/shard_map/ppermute | solution.py:35
  58.3 5.8 %collective-permute-done.14.b_ref = bf16[464,128]{1,0:T(8,128)(2,1)S(1)} collective-permute-done((bf16[464,128]{1,0:T(8,128)(2,1)}, bf16[464,128]{1,0:T(8,128)(2,1)S(1)}, u32[]{:S(2)}, u32[]{:S(2)}) %collective-permute-start.14) | collective-permute-done | bytes 118816 | tf_op jit(solution)/shard_map/ppermute | solution.py:35
  64.1 0.6 copy-done.4
  64.8 1.6 %shard_map.116 = (bf16[432,128]{1,0:T(8,128)(2,1)}, f32[8,128]{1,0:T(8,128)}) custom-call(bf16[464,128]{1,0:T(8,128)(2,1)} %shard_map.115.a_ref, bf16[464,128]{1,0:T(8,128)(2,1)} %copy-done.4), custom_call_target="tpu_custom_call" | custom-call | flops 1000000 | bytes 352256 | tf_op jit(solution)/shard_map/pallas_call | solution.py:19
  66.4 1.2 %collective-permute-start.15 = (bf16[432,128]{1,0:T(8,128)(2,1)}, bf16[432,128]{1,0:T(8,128)(2,1)S(1)}, u32[]{:S(2)}, u32[]{:S(2)}) collective-permute-start(bf16[432,128]{1,0:T(8,128)(2,1)} %get-tuple-element.40.own_ref), channel_id=1, source_target_pairs={{0,8},{8,0},{16,24},{24,16},{1,9},{9,1},{17,25},{25,17},{2,10},{10... | collective-permute-start | bytes 331784 | tf_op jit(solution)/shard_map/ppermute | solution.py:35
  67.6 0.9 collective-permute-start.16
  68.5 1.4 %collective-permute-start.17 = (bf16[432,128]{1,0:T(8,128)(2,1)}, bf16[432,128]{1,0:T(8,128)(2,1)S(1)}, u32[]{:S(2)}, u32[]{:S(2)}) collective-permute-start(bf16[432,128]{1,0:T(8,128)(2,1)} %get-tuple-element.40.own_ref), channel_id=1, source_target_pairs={{0,24},{8,16},{16,8},{24,0},{1,25},{9,17},{17,9},{25,1},{2,26},{10... | collective-permute-start | bytes 331784 | tf_op jit(solution)/shard_map/ppermute | solution.py:35
  69.9 1.5 %collective-permute-done.15.rest_0_ = bf16[432,128]{1,0:T(8,128)(2,1)S(1)} collective-permute-done((bf16[432,128]{1,0:T(8,128)(2,1)}, bf16[432,128]{1,0:T(8,128)(2,1)S(1)}, u32[]{:S(2)}, u32[]{:S(2)}) %collective-permute-start.15) | collective-permute-done | bytes 110624 | tf_op jit(solution)/shard_map/ppermute | solution.py:35
  71.4 1.2 %collective-permute-done.16.rest_1_ = bf16[432,128]{1,0:T(8,128)(2,1)S(1)} collective-permute-done((bf16[432,128]{1,0:T(8,128)(2,1)}, bf16[432,128]{1,0:T(8,128)(2,1)S(1)}, u32[]{:S(2)}, u32[]{:S(2)}) %collective-permute-start.16) | collective-permute-done | bytes 110624 | tf_op jit(solution)/shard_map/ppermute | solution.py:35
  72.6 1.8 %collective-permute-done.17.rest_2_ = bf16[432,128]{1,0:T(8,128)(2,1)S(1)} collective-permute-done((bf16[432,128]{1,0:T(8,128)(2,1)}, bf16[432,128]{1,0:T(8,128)(2,1)S(1)}, u32[]{:S(2)}, u32[]{:S(2)}) %collective-permute-start.17) | collective-permute-done | bytes 110624 | tf_op jit(solution)/shard_map/ppermute | solution.py:35
  74.3 0.6 copy-done.10
  75.0 1.9 %shard_map.118.own_ref = bf16[1728,128]{1,0:T(8,128)(2,1)} custom-call(bf16[432,128]{1,0:T(8,128)(2,1)} %get-tuple-element.40.own_ref, bf16[432,128]{1,0:T(8,128)(2,1)} %copy-done.8, bf16[432,128]{1,0:T(8,128)(2,1)} %copy-done.9, bf16[432,128]{1,0:T(8,128)(2,1)} %copy-done.10), custom_call_target="tpu_custom_call" | custom-call | flops 1000000 | bytes 884736 | tf_op jit(solution)/shard_map/pallas_call | solution.py:19
  76.8 2.3 %collective-permute-start = (bf16[2,4,160,128]{3,2,1,0:T(8,128)(2,1)S(1)}, bf16[2,4,160,128]{3,2,1,0:T(8,128)(2,1)S(1)}, u32[]{:S(2)}, u32[]{:S(2)}) collective-permute-start(bf16[2,4,160,128]{3,2,1,0:T(8,128)(2,1)S(1)} %bitcast.18), channel_id=1, source_target_pairs={{0,2},{1,3},{2,4},{3,5},{4,6},{5,7},{8,10},{9,11},{10,12},{11,13},... | collective-permute-start | bytes 983048 | tf_op jit(solution)/shard_map/ppermute | solution.py:45
  79.1 0.3 collective-permute-start.7
  79.4 2.1 %collective-permute-start.8 = (bf16[2,160,128]{2,1,0:T(8,128)(2,1)S(1)}, bf16[2,160,128]{2,1,0:T(8,128)(2,1)S(1)}, u32[]{:S(2)}, u32[]{:S(2)}) collective-permute-start(bf16[2,160,128]{2,1,0:T(8,128)(2,1)S(1)} %dynamic-slice_bitcast_fusion), channel_id=1, source_target_pairs={{1,2},{0,3},{3,4},{2,5},{5,6},{4,7},{9,10},{8,11},{11,12},{10,13},... | collective-permute-start | bytes 245768 | tf_op jit(solution)/shard_map/ppermute | solution.py:55
  81.6 6.9 %collective-permute-done.8.rest_1_ = bf16[2,160,128]{2,1,0:T(8,128)(2,1)S(1)} collective-permute-done((bf16[2,160,128]{2,1,0:T(8,128)(2,1)S(1)}, bf16[2,160,128]{2,1,0:T(8,128)(2,1)S(1)}, u32[]{:S(2)}, u32[]{:S(2)}) %collective-permute-start.8) | collective-permute-done | bytes 81952 | tf_op jit(solution)/shard_map/ppermute | solution.py:55
  88.5 0.6 copy-done.17
  89.2 5.1 %shard_map.112 = bf16[2,8,320,128]{3,2,1,0:T(8,128)(2,1)} custom-call(bf16[2,4,160,128]{3,2,1,0:T(8,128)(2,1)} %bitcast.16, bf16[2,4,160,128]{3,2,1,0:T(8,128)(2,1)} %copy-done.13, f32[8,128]{1,0:T(8,128)} %get-tuple-element.28.norm_ref, bf16[3,3,384,128]{3,2,1,0:T(8,128)(2,1)} %kernel_ref.3, f32[1,128]{1,0:T(1,128)} %bitcast.21, f32[1,128]{1,0:T(1,128)} %bitcast.25, ...), custom_call_target="tpu_custom_call" | custom-call | flops 1132462080 | bytes 3020288 | tf_op jit(solution)/shard_map/pallas_call | solution.py:19
  94.3 2.2 %shard_map.117 = (bf16[2,4,160,128]{3,2,1,0:T(8,128)(2,1)}, f32[1,128]{1,0:T(1,128)}, f32[1,128]{1,0:T(1,128)}, f32[1,128]{1,0:T(1,128)}) custom-call(f32[2,4,160,128]{3,2,1,0:T(8,128)} %get-tuple-element.29.dpre_ref, bf16[2,4,160,128]{3,2,1,0:T(8,128)(2,1)} %bitcast.17, f32[8,128]{1,0:T(8,128)} %get-tuple-element.28.norm_ref, ...), custom_call_target="tpu_custom_call" | custom-call | flops 1000000 | bytes 1320960 | tf_op jit(solution)/shard_map/pallas_call | solution.py:19
  96.5 0.8 copy-done.2
  97.3 2.5 %shard_map.119 = f32[3456,128]{1,0:T(8,128)} custom-call(bf16[1728,128]{1,0:T(8,128)(2,1)} %shard_map.118.own_ref, bf16[1728,128]{1,0:T(8,128)(2,1)} %copy-done.2), custom_call_target="tpu_custom_call" | custom-call | flops 1000000 | bytes 2654208 | tf_op jit(solution)/shard_map/pallas_call | solution.py:19
  (46 shorter events, 0.5 us)
Async XLA Ops:
  2.4 1.5 %collective-permute-start.1 = (f32[8,128]{1,0:T(8,128)}, f32[8,128]{1,0:T(8,128)S(1)}, u32[]{:S(2)}, u32[]{:S(2)}) collective-permute-start(f32[8,128]{1,0:T(8,128)} %shard_map.109), channel_id=1, source_target_pairs={{0,1},{1,0},{2,3},{3,2},{4,5},{5,4},{6,7},{7,6},{8,9},{9,8},{10,11... | collective-permute-start | bytes 12296 | tf_op jit(solution)/shard_map/ppermute | solution.py:35
  4.7 7.8 %collective-permute-start.2 = (f32[8,128]{1,0:T(8,128)S(1)}, f32[8,128]{1,0:T(8,128)S(1)}, u32[]{:S(2)}, u32[]{:S(2)}) collective-permute-start(f32[8,128]{1,0:T(8,128)S(1)} %maximum_maximum_fusion), channel_id=1, source_target_pairs={{0,2},{2,0},{4,6},{6,4},{1,3},{3,1},{5,7},{7,5},{8,10},{10,8},{12,... | collective-permute-start | bytes 12296 | tf_op jit(solution)/shard_map/ppermute | solution.py:35
  10.0 15.3 %collective-permute-start.5 = (bf16[2,160,128]{2,1,0:T(8,128)(2,1)}, bf16[2,160,128]{2,1,0:T(8,128)(2,1)S(1)}, u32[]{:S(2)}, u32[]{:S(2)}) collective-permute-start(bf16[2,160,128]{2,1,0:T(8,128)(2,1)} %get-tuple-element.27), channel_id=1, source_target_pairs={{1,0},{0,1},{3,2},{2,3},{5,4},{4,5},{7,6},{6,7},{9,8},{8,9},{11,10... | collective-permute-start | bytes 245768 | tf_op jit(solution)/shard_map/ppermute | solution.py:55
  10.0 15.3 %collective-permute-start.6 = (bf16[2,160,128]{2,1,0:T(8,128)(2,1)}, bf16[2,160,128]{2,1,0:T(8,128)(2,1)S(1)}, u32[]{:S(2)}, u32[]{:S(2)}) collective-permute-start(bf16[2,160,128]{2,1,0:T(8,128)(2,1)} %get-tuple-element.27), channel_id=1, source_target_pairs={{3,0},{2,1},{5,2},{4,3},{7,4},{6,5},{11,8},{10,9},{13,10},{12,11},... | collective-permute-start | bytes 245768 | tf_op jit(solution)/shard_map/ppermute | solution.py:55
  11.2 14.0 %collective-permute-start.4 = (bf16[2,4,160,128]{3,2,1,0:T(8,128)(2,1)}, bf16[2,4,160,128]{3,2,1,0:T(8,128)(2,1)S(1)}, u32[]{:S(2)}, u32[]{:S(2)}) collective-permute-start(bf16[2,4,160,128]{3,2,1,0:T(8,128)(2,1)} %get-tuple-element.25.grad_ref), channel_id=1, source_target_pairs={{2,0},{3,1},{4,2},{5,3},{6,4},{7,5},{10,8},{11,9},{12,10},{13,11},... | collective-permute-start | bytes 983048 | tf_op jit(solution)/shard_map/ppermute | solution.py:45
  12.6 12.7 %copy-start.11 = (f32[8,128]{1,0:T(8,128)}, f32[8,128]{1,0:T(8,128)S(1)}, u32[]{:S(2)}) copy-start(f32[8,128]{1,0:T(8,128)S(1)} %maximum_maximum_fusion.1.mine_ref) | copy-start | bytes 12292
  12.6 12.6 %collective-permute-start.3 = (f32[8,128]{1,0:T(8,128)S(1)}, f32[8,128]{1,0:T(8,128)S(1)}, u32[]{:S(2)}, u32[]{:S(2)}) collective-permute-start(f32[8,128]{1,0:T(8,128)S(1)} %maximum_maximum_fusion.1.mine_ref), channel_id=1, source_target_pairs={{0,4},{2,6},{4,0},{6,2},{1,5},{3,7},{5,1},{7,3},{8,12},{10,14},{12... | collective-permute-start | bytes 12296 | tf_op jit(solution)/shard_map/ppermute | solution.py:35
  25.2 0.6 copy-start.18
  25.3 0.6 copy-start.14
  25.3 0.7 copy-start.15
  25.3 0.8 copy-start.12
  32.8 2.0 %collective-permute-start.9 = (bf16[1760,128]{1,0:T(8,128)(2,1)}, bf16[1760,128]{1,0:T(8,128)(2,1)S(1)}, u32[]{:S(2)}, u32[]{:S(2)}) collective-permute-start(bf16[1760,128]{1,0:T(8,128)(2,1)} %get-tuple-element.32), channel_id=1, source_target_pairs={{0,1},{1,0},{2,3},{3,2},{4,5},{5,4},{6,7},{7,6},{8,9},{9,8},{10,11... | collective-permute-start | bytes 1351688 | tf_op jit(solution)/shard_map/ppermute | solution.py:35
  34.8 0.8 copy-start.1
  37.8 39.0 %copy-start = (bf16[1,2,4,160,128]{4,3,2,1,0:T(8,128)(2,1)S(1)}, bf16[1,2,4,160,128]{4,3,2,1,0:T(8,128)(2,1)}, u32[]{:S(2)}) copy-start(bf16[1,2,4,160,128]{4,3,2,1,0:T(8,128)(2,1)} %param.6) | copy-start | bytes 983044
  37.8 5.6 %collective-permute-start.10 = (bf16[464,128]{1,0:T(8,128)(2,1)}, bf16[464,128]{1,0:T(8,128)(2,1)S(1)}, u32[]{:S(2)}, u32[]{:S(2)}) collective-permute-start(bf16[464,128]{1,0:T(8,128)(2,1)} %get-tuple-element.35), channel_id=1, source_target_pairs={{0,8},{8,0},{16,24},{24,16},{1,9},{9,1},{17,25},{25,17},{2,10},{10... | collective-permute-start | bytes 356360 | tf_op jit(solution)/shard_map/ppermute | solution.py:35
  39.3 7.8 %collective-permute-start.11 = (bf16[464,128]{1,0:T(8,128)(2,1)}, bf16[464,128]{1,0:T(8,128)(2,1)S(1)}, u32[]{:S(2)}, u32[]{:S(2)}) collective-permute-start(bf16[464,128]{1,0:T(8,128)(2,1)} %get-tuple-element.36), channel_id=1, source_target_pairs={{0,16},{8,24},{16,0},{24,8},{1,17},{9,25},{17,1},{25,9},{2,18},{10... | collective-permute-start | bytes 356360 | tf_op jit(solution)/shard_map/ppermute | solution.py:35
  40.8 6.2 %collective-permute-start.12 = (bf16[464,128]{1,0:T(8,128)(2,1)}, bf16[464,128]{1,0:T(8,128)(2,1)S(1)}, u32[]{:S(2)}, u32[]{:S(2)}) collective-permute-start(bf16[464,128]{1,0:T(8,128)(2,1)} %get-tuple-element.37), channel_id=1, source_target_pairs={{0,24},{8,16},{16,8},{24,0},{1,25},{9,17},{17,9},{25,1},{2,26},{10... | collective-permute-start | bytes 356360 | tf_op jit(solution)/shard_map/ppermute | solution.py:35
  43.4 3.6 %copy-start.5 = (bf16[464,128]{1,0:T(8,128)(2,1)}, bf16[464,128]{1,0:T(8,128)(2,1)S(1)}, u32[]{:S(2)}) copy-start(bf16[464,128]{1,0:T(8,128)(2,1)S(1)} %collective-permute-done.10.rest_0_) | copy-start | bytes 356356
  47.0 0.7 copy-start.6
  47.0 0.7 copy-start.7
  49.6 5.0 %collective-permute-start.13 = (bf16[464,128]{1,0:T(8,128)(2,1)}, bf16[464,128]{1,0:T(8,128)(2,1)S(1)}, u32[]{:S(2)}, u32[]{:S(2)}) collective-permute-start(bf16[464,128]{1,0:T(8,128)(2,1)} %shard_map.114.a_ref), channel_id=1, source_target_pairs={{0,2},{2,0},{4,6},{6,4},{1,3},{3,1},{5,7},{7,5},{8,10},{10,8},{12,... | collective-permute-start | bytes 356360 | tf_op jit(solution)/shard_map/ppermute | solution.py:35
  54.6 0.6 copy-start.3
  56.9 7.2 %collective-permute-start.14 = (bf16[464,128]{1,0:T(8,128)(2,1)}, bf16[464,128]{1,0:T(8,128)(2,1)S(1)}, u32[]{:S(2)}, u32[]{:S(2)}) collective-permute-start(bf16[464,128]{1,0:T(8,128)(2,1)} %shard_map.115.a_ref), channel_id=1, source_target_pairs={{0,4},{2,6},{4,0},{6,2},{1,5},{3,7},{5,1},{7,3},{8,12},{10,14},{12... | collective-permute-start | bytes 356360 | tf_op jit(solution)/shard_map/ppermute | solution.py:35
  64.1 0.6 copy-start.4
  66.4 5.0 %collective-permute-start.15 = (bf16[432,128]{1,0:T(8,128)(2,1)}, bf16[432,128]{1,0:T(8,128)(2,1)S(1)}, u32[]{:S(2)}, u32[]{:S(2)}) collective-permute-start(bf16[432,128]{1,0:T(8,128)(2,1)} %get-tuple-element.40.own_ref), channel_id=1, source_target_pairs={{0,8},{8,0},{16,24},{24,16},{1,9},{9,1},{17,25},{25,17},{2,10},{10... | collective-permute-start | bytes 331784 | tf_op jit(solution)/shard_map/ppermute | solution.py:35
  67.6 5.0 %collective-permute-start.16 = (bf16[432,128]{1,0:T(8,128)(2,1)}, bf16[432,128]{1,0:T(8,128)(2,1)S(1)}, u32[]{:S(2)}, u32[]{:S(2)}) collective-permute-start(bf16[432,128]{1,0:T(8,128)(2,1)} %get-tuple-element.40.own_ref), channel_id=1, source_target_pairs={{0,16},{8,24},{16,0},{24,8},{1,17},{9,25},{17,1},{25,9},{2,18},{10... | collective-permute-start | bytes 331784 | tf_op jit(solution)/shard_map/ppermute | solution.py:35
  68.5 5.9 %collective-permute-start.17 = (bf16[432,128]{1,0:T(8,128)(2,1)}, bf16[432,128]{1,0:T(8,128)(2,1)S(1)}, u32[]{:S(2)}, u32[]{:S(2)}) collective-permute-start(bf16[432,128]{1,0:T(8,128)(2,1)} %get-tuple-element.40.own_ref), channel_id=1, source_target_pairs={{0,24},{8,16},{16,8},{24,0},{1,25},{9,17},{17,9},{25,1},{2,26},{10... | collective-permute-start | bytes 331784 | tf_op jit(solution)/shard_map/ppermute | solution.py:35
  71.4 3.0 %copy-start.8 = (bf16[432,128]{1,0:T(8,128)(2,1)}, bf16[432,128]{1,0:T(8,128)(2,1)S(1)}, u32[]{:S(2)}) copy-start(bf16[432,128]{1,0:T(8,128)(2,1)S(1)} %collective-permute-done.15.rest_0_) | copy-start | bytes 331780
  72.6 1.8 %copy-start.9 = (bf16[432,128]{1,0:T(8,128)(2,1)}, bf16[432,128]{1,0:T(8,128)(2,1)S(1)}, u32[]{:S(2)}) copy-start(bf16[432,128]{1,0:T(8,128)(2,1)S(1)} %collective-permute-done.16.rest_1_) | copy-start | bytes 331780
  74.3 0.6 copy-start.10
  76.8 19.7 %collective-permute-start.18 = (bf16[1728,128]{1,0:T(8,128)(2,1)}, bf16[1728,128]{1,0:T(8,128)(2,1)S(1)}, u32[]{:S(2)}, u32[]{:S(2)}) collective-permute-start(bf16[1728,128]{1,0:T(8,128)(2,1)} %shard_map.118.own_ref), channel_id=1, source_target_pairs={{0,1},{1,0},{2,3},{3,2},{4,5},{5,4},{6,7},{7,6},{8,9},{9,8},{10,11... | collective-permute-start | bytes 1327112 | tf_op jit(solution)/shard_map/ppermute | solution.py:35
  76.8 11.6 %collective-permute-start = (bf16[2,4,160,128]{3,2,1,0:T(8,128)(2,1)S(1)}, bf16[2,4,160,128]{3,2,1,0:T(8,128)(2,1)S(1)}, u32[]{:S(2)}, u32[]{:S(2)}) collective-permute-start(bf16[2,4,160,128]{3,2,1,0:T(8,128)(2,1)S(1)} %bitcast.18), channel_id=1, source_target_pairs={{0,2},{1,3},{2,4},{3,5},{4,6},{5,7},{8,10},{9,11},{10,12},{11,13},... | collective-permute-start | bytes 983048 | tf_op jit(solution)/shard_map/ppermute | solution.py:45
  79.1 2.4 %collective-permute-start.7 = (bf16[2,160,128]{2,1,0:T(8,128)(2,1)S(1)}, bf16[2,160,128]{2,1,0:T(8,128)(2,1)S(1)}, u32[]{:S(2)}, u32[]{:S(2)}) collective-permute-start(bf16[2,160,128]{2,1,0:T(8,128)(2,1)S(1)} %dynamic-slice_bitcast_fusion), channel_id=1, source_target_pairs={{1,0},{0,1},{3,2},{2,3},{5,4},{4,5},{7,6},{6,7},{9,8},{8,9},{11,10... | collective-permute-start | bytes 245768 | tf_op jit(solution)/shard_map/ppermute | solution.py:55
  79.4 9.0 %collective-permute-start.8 = (bf16[2,160,128]{2,1,0:T(8,128)(2,1)S(1)}, bf16[2,160,128]{2,1,0:T(8,128)(2,1)S(1)}, u32[]{:S(2)}, u32[]{:S(2)}) collective-permute-start(bf16[2,160,128]{2,1,0:T(8,128)(2,1)S(1)} %dynamic-slice_bitcast_fusion), channel_id=1, source_target_pairs={{1,2},{0,3},{3,4},{2,5},{5,6},{4,7},{9,10},{8,11},{11,12},{10,13},... | collective-permute-start | bytes 245768 | tf_op jit(solution)/shard_map/ppermute | solution.py:55
  81.6 6.9 %copy-start.16 = (bf16[2,160,128]{2,1,0:T(8,128)(2,1)}, bf16[2,160,128]{2,1,0:T(8,128)(2,1)S(1)}, u32[]{:S(2)}) copy-start(bf16[2,160,128]{2,1,0:T(8,128)(2,1)S(1)} %collective-permute-done.7.rest_0_) | copy-start | bytes 245764
  88.5 0.6 copy-start.17
  88.5 0.7 copy-start.13
  96.5 0.8 copy-start.2

commit v2 on v1

--- a/solution.py
+++ b/solution.py
@@ -1,4 +1,5 @@
 import functools
+import math
 
 import jax
 import jax.numpy as jnp
@@ -14,14 +15,16 @@
 VMEM = pl.BlockSpec(memory_space=pltpu.VMEM)
 
 
-def call(body, outs, *args, scratch=(), flops=1_000_000):
+def call(body, outs, *args, scratch=(), flops=1_000_000, room=2 << 20):
     moved = sum(a.size * a.dtype.itemsize for a in (*args, *outs))
+    held = sum(math.prod(s.shape) * jnp.dtype(s.dtype).itemsize for s in scratch)
     return pl.pallas_call(
         body,
         out_shape=tuple(outs),
         in_specs=[VMEM] * len(args),
         out_specs=tuple([VMEM] * len(outs)),
         scratch_shapes=list(scratch),
+        compiler_params=pltpu.CompilerParams(vmem_limit_bytes=moved + held + room),
         cost_estimate=pl.CostEstimate(flops=flops, bytes_accessed=moved, transcendentals=0),
     )(*args)
 
@@ -98,23 +101,6 @@
     return jnp.where(row == x.shape[0] - 1, x if edge else 0.0, pltpu.roll(x, x.shape[0] - 1, 0))
 
 
-def stats_body(lat_ref, out_ref):
-    t_n, r_n, w_n, c_n = lat_ref.shape
-    total = jnp.zeros((8, c_n), F32)
-    for t in range(t_n):
-        for r in range(r_n):
-            total += jnp.sum(lat_ref[t, r].astype(F32).reshape(w_n // 8, 8, c_n), axis=0)
-    mean = jnp.sum(total, axis=0, keepdims=True) / (t_n * r_n * w_n)
-    square = jnp.zeros((8, c_n), F32)
-    for t in range(t_n):
-        for r in range(r_n):
-            x = (lat_ref[t, r].astype(F32) - mean).reshape(w_n // 8, 8, c_n)
-            square += jnp.sum(x * x, axis=0)
-    square = jnp.sum(square, axis=0, keepdims=True)
-    row = lax.broadcasted_iota(jnp.int32, (8, c_n), 0)
-    out_ref[...] = jnp.where(row == 0, mean, jnp.where(row == 1, square, 0.0))
-
-
 def fold_body(edge_n, cot_ref, out_ref, bias_ref, *rest):
     edge_refs, wide = rest[:edge_n], rest[edge_n]
     t_n, r2, w2, c_n = cot_ref.shape
@@ -128,65 +114,80 @@
             total += jnp.sum(value.reshape(w_n // 8, 8, c_n), axis=0)
             out_ref[t, r] = value.astype(BF16)
     bias_ref[...] = jnp.broadcast_to(jnp.sum(total, axis=0, keepdims=True), (8, c_n))
-    edges(out_ref, edge_refs, r_n)
-
-
-def edges(ref, edge_refs, r_n):
-    if len(edge_refs) == 1:
-        row = jnp.where(lax.axis_index("height") == 0, r_n - 1, 0)
-        edge_refs[0][...] = ref[:, row]
+    for ref, row in zip(edge_refs, facing_rows(edge_n, r_n)):
+        ref[...] = out_ref[:, row]
+
+
+def facing_rows(edge_n, r_n):
+    if edge_n == 1:
+        return [jnp.where(lax.axis_index("height") == 0, r_n - 1, 0)]
+    return [r_n - 1, 0]
+
+
+def stats_body(edge_n, lat_ref, grad_ref, out_ref, *edge_refs):
+    t_n, r_n, w_n, c_n = lat_ref.shape
+    total = jnp.zeros((8, c_n), F32)
+    for t in range(t_n):
+        for r in range(r_n):
+            total += jnp.sum(lat_ref[t, r].astype(F32).reshape(w_n // 8, 8, c_n), axis=0)
+    mean = jnp.sum(total, axis=0, keepdims=True) / (t_n * r_n * w_n)
+    square = jnp.zeros((8, c_n), F32)
+    for t in range(t_n):
+        for r in range(r_n):
+            x = (lat_ref[t, r].astype(F32) - mean).reshape(w_n // 8, 8, c_n)
+            square += jnp.sum(x * x, axis=0)
+    square = jnp.sum(square, axis=0, keepdims=True)
+    row = lax.broadcasted_iota(jnp.int32, (8, c_n), 0)
+    stats = jnp.where(row == 0, mean, jnp.where(row == 1, square, 0.0))
+    out_ref[...] = stats
+    for ref, row in zip(edge_refs, facing_rows(edge_n, r_n)):
+        for t in range(t_n):
+            ref[pl.ds(t * w_n, w_n), :] = lat_ref[t, row]
+            ref[pl.ds((t_n + t) * w_n, w_n), :] = grad_ref[t, row]
+        ref[pl.ds(2 * t_n * w_n, TAB), :] = packed(stats)
+
+
+def merged(a, b, cells):
+    gap = a[0:1] - b[0:1]
+    return (a[0:1] + b[0:1]) * 0.5, a[1:2] + b[1:2] + gap * gap * (cells / 4)
+
+
+def merge_body(cells, a_ref, b_ref, out_ref):
+    a = a_ref[...]
+    if b_ref.shape[0] == 8:
+        b = b_ref[...]
     else:
-        edge_refs[0][...] = ref[:, r_n - 1]
-        edge_refs[1][...] = ref[:, 0]
-
-
-def main_body(
-    n_edge, cells, n_h,
-    lat_ref, mine_ref, other_ref, grad_ref, halo_ref, kernel_ref, gain_ref, shift_ref, bias_ref, *rest,
-):
+        a = unpacked(packed(a))
+        b = unpacked(b_ref[b_ref.shape[0] - TAB :])
+    mean, square = merged(a, b, cells)
+    row = lax.broadcasted_iota(jnp.int32, a.shape, 0)
+    out_ref[...] = jnp.where(row == 0, mean, jnp.where(row == 1, square, 0.0))
+
+
+def back_body(n_edge, n_h, lat_ref, stats_ref, grad_ref, halo_ref, kernel_ref, *rest):
     edge_refs, corner_refs, rest = rest[:n_edge], rest[n_edge : 2 * n_edge], rest[2 * n_edge :]
-    keep_ref, table_ref, dpre_ref, norm_ref = rest[:4]
-    send_refs, (acts, fold, weight, slope, hats, sums) = rest[4 : 3 + n_h], rest[3 + n_h :]
+    fold, dact_ref, lead_ref, weight = rest
     t_n, r_n, w_n, c_n = lat_ref.shape
     h = lax.axis_index("height")
     top = (h == 0).astype(F32)
     bottom = (h == n_h - 1).astype(F32)
     first = (lax.axis_index("tm") == 0).astype(F32)
 
-    a, b = mine_ref[...], other_ref[...]
-    gap = a[0:1] - b[0:1]
-    channel_mean = (a[0:1] + b[0:1]) * 0.5
-    square = a[1:2] + b[1:2] + gap * gap * (cells / 4)
-    channel_mean = jnp.broadcast_to(channel_mean, (8, c_n))
-    size = c_n // GROUPS
-    mean = group_sum(channel_mean) * (1.0 / size)
-    off = channel_mean - mean
-    var = group_sum(jnp.broadcast_to(square, (8, c_n)) + off * off * cells) * (1.0 / (cells * size))
-    rstd = lax.rsqrt(var + 1e-06)
-    row = lax.broadcasted_iota(jnp.int32, (8, c_n), 0)
-    norm_ref[...] = jnp.where(row == 0, mean, rstd)
-    mean, rstd = mean[0:1], rstd[0:1]
-    gain, shift = gain_ref[...], shift_ref[...]
-
-    for t in range(t_n):
-        for r in range(r_n):
-            at = pl.ds((t * r_n + r) * w_n, w_n)
-            hat = (lat_ref[t, r].astype(F32) - mean) * rstd
-            pre = hat * gain + shift
-            sig = jax.nn.sigmoid(pre)
-            act = pre * sig
-            hats[at, :] = hat
-            slope[at, :] = sig * (1.0 + pre * (1.0 - sig))
-            acts[at, 0:c_n] = before(act, True).astype(BF16)
-            acts[at, c_n : 2 * c_n] = act.astype(BF16)
-            acts[at, 2 * c_n :] = after(act, True).astype(BF16)
+    for t in range(t_n):
+        for r in range(r_n):
+            lead_ref[t, r] = lat_ref[t, r]
+        for e, ref in enumerate(edge_refs):
+            lead_ref[t, r_n + e] = ref[pl.ds(t * w_n, w_n), :]
 
     def source(f, r):
         if 0 <= r < r_n:
             return (grad_ref[f, r] if f < t_n else halo_ref[f - t_n, r]).astype(F32)
-        refs = edge_refs if f < t_n else corner_refs
-        ref = refs[0] if r < 0 else refs[-1]
-        return ref[f % t_n].astype(F32) * ((1.0 - top) if r < 0 else (1.0 - bottom))
+        which = 0 if r < 0 else -1
+        if f < t_n:
+            value = edge_refs[which][pl.ds((t_n + f) * w_n, w_n), :]
+        else:
+            value = corner_refs[which][f - t_n]
+        return value.astype(F32) * ((1.0 - top) if r < 0 else (1.0 - bottom))
 
     for j in range(3):
         for r in range(r_n):
@@ -206,8 +207,67 @@
                         value = value + first * (frame[0] + frame[1] if i == 0 else frame[0])
                     fold[pl.ds((t * r_n + r) * w_n, w_n), lanes] = value.astype(BF16)
 
+    for ij in range(9):
+        weight[:, ij * c_n : (ij + 1) * c_n] = kernel_ref[ij // 3, ij % 3]
+    for t in range(t_n):
+        back = lax.dot_general(
+            fold[pl.ds(t * r_n * w_n, r_n * w_n), :], weight[...], (((1,), (1,)), ((), ())),
+            preferred_element_type=F32,
+        )
+        for r in range(r_n):
+            slab = back[r * w_n : (r + 1) * w_n]
+            low, mid, high = (slab[:, k * c_n : (k + 1) * c_n] for k in range(3))
+            col = lax.broadcasted_iota(jnp.int32, low.shape, 0)
+            dact_ref[t, r] = (
+                mid + after(low, False) + before(high, False)
+                + jnp.where(col == 0, low, 0.0) + jnp.where(col == w_n - 1, high, 0.0)
+            )
+
+
+def main_body(
+    cells, n_h,
+    lat_ref, mine_ref, other_ref, fold_ref, dact_ref, gain_ref, shift_ref, bias_ref, *rest,
+):
+    keep_ref, table_ref, dpre_ref, norm_ref = rest[:4]
+    send_refs, (acts, sums) = rest[4 : 3 + n_h], rest[3 + n_h :]
+    t_n, r_n, w_n, c_n = lat_ref.shape
+    h = lax.axis_index("height")
+
+    channel_mean, square = merged(mine_ref[...], other_ref[...], cells)
+    channel_mean = jnp.broadcast_to(channel_mean, (8, c_n))
+    size = c_n // GROUPS
+    mean = group_sum(channel_mean) * (1.0 / size)
+    off = channel_mean - mean
+    var = group_sum(jnp.broadcast_to(square, (8, c_n)) + off * off * cells) * (1.0 / (cells * size))
+    rstd = lax.rsqrt(var + 1e-06)
+    row = lax.broadcasted_iota(jnp.int32, (8, c_n), 0)
+    norm_ref[...] = jnp.where(row == 0, mean, rstd)
+    mean, rstd = mean[0:1], rstd[0:1]
+    gain, shift = gain_ref[...], shift_ref[...]
+
+    total_a = jnp.zeros((8, c_n), F32)
+    total_b = jnp.zeros((8, c_n), F32)
+    for t in range(t_n):
+        for r in range(r_n):
+            at = pl.ds((t * r_n + r) * w_n, w_n)
+            hat = (lat_ref[t, r].astype(F32) - mean) * rstd
+            pre = hat * gain + shift
+            sig = jax.nn.sigmoid(pre)
+            act = pre * sig
+            acts[at, 0:c_n] = before(act, True).astype(BF16)
+            acts[at, c_n : 2 * c_n] = act.astype(BF16)
+            acts[at, 2 * c_n :] = after(act, True).astype(BF16)
+            dpre = dact_ref[t, r] * sig * (1.0 + pre * (1.0 - sig))
+            dpre_ref[t, r] = dpre
+            total_a += jnp.sum((dpre * hat).reshape(w_n // 8, 8, c_n), axis=0)
+            total_b += jnp.sum(dpre.reshape(w_n // 8, 8, c_n), axis=0)
+    total_a = jnp.sum(total_a, axis=0, keepdims=True)
+    total_b = jnp.sum(total_b, axis=0, keepdims=True)
+    table = jnp.where(row == 0, bias_ref[...], jnp.where(row == 1, total_a, jnp.where(row == 2, total_b, 0.0)))
+    table_ref[...] = table
+
     product = lax.dot_general(
-        acts[...], fold[...], (((0,), (0,)), ((), ())), preferred_element_type=F32
+        acts[...], fold_ref[...], (((0,), (0,)), ((), ())), preferred_element_type=F32
     )
     for ij in range(9):
         sums[pl.ds(ij * 3 * c_n, 3 * c_n), :] = product[:, ij * c_n : (ij + 1) * c_n]
@@ -217,34 +277,6 @@
     keep_ref[...] = sums[pl.ds(h * share, share), :]
     for s, ref in enumerate(send_refs, 1):
         ref[0:share] = sums[pl.ds((h ^ s) * share, share), :].astype(BF16)
-
-    for ij in range(9):
-        weight[:, ij * c_n : (ij + 1) * c_n] = kernel_ref[ij // 3, ij % 3]
-    total_a = jnp.zeros((8, c_n), F32)
-    total_b = jnp.zeros((8, c_n), F32)
-    for t in range(t_n):
-        back = lax.dot_general(
-            fold[pl.ds(t * r_n * w_n, r_n * w_n), :], weight[...], (((1,), (1,)), ((), ())),
-            preferred_element_type=F32,
-        )
-        for r in range(r_n):
-            slab = back[r * w_n : (r + 1) * w_n]
-            low, mid, high = (slab[:, k * c_n : (k + 1) * c_n] for k in range(3))
-            col = lax.broadcasted_iota(jnp.int32, low.shape, 0)
-            dact = (
-                mid + after(low, False) + before(high, False)
-                + jnp.where(col == 0, low, 0.0) + jnp.where(col == w_n - 1, high, 0.0)
-            )
-            at = pl.ds((t * r_n + r) * w_n, w_n)
-            dpre = dact * slope[at, :]
-            dpre_ref[t, r] = dpre
-            total_a += jnp.sum((dpre * hats[at, :]).reshape(w_n // 8, 8, c_n), axis=0)
-            total_b += jnp.sum(dpre.reshape(w_n // 8, 8, c_n), axis=0)
-    total_a = jnp.sum(total_a, axis=0, keepdims=True)
-    total_b = jnp.sum(total_b, axis=0, keepdims=True)
-    table = jnp.where(row == 0, bias_ref[...], jnp.where(row == 1, total_a, jnp.where(row == 2, total_b, 0.0)))
-    table_ref[...] = table
-    for ref in send_refs:
         ref[share:] = packed(table)
 
 
@@ -265,7 +297,7 @@
         ref[piece:] = packed(table)
 
 
-def second_sum_body(own_ref, table_ref, *rest):
+def second_sum_body(own_ref, table_ref, token_ref, *rest):
     got, out_ref = rest[:-1], rest[-1]
     piece = own_ref.shape[0]
     value = own_ref[...]
@@ -291,7 +323,7 @@
     table_ref[...] = unpacked(a_ref[piece:]) + unpacked(b_ref[piece:])
 
 
-def gather_body(own_ref, *rest):
+def gather_body(token_ref, own_ref, *rest):
     got, out_ref = rest[:-1], rest[-1]
     piece = own_ref.shape[0]
     me = lax.axis_index("dp")
@@ -315,10 +347,11 @@
 
 def forward_body(
     n_edge, n_h,
-    lat_ref, past_ref, norm_ref, kernel_ref, gain_ref, shift_ref, offset_ref, *rest,
+    lat_ref, past_ref, norm_ref, kernel_ref, gain_ref, shift_ref, offset_ref, after_ref, *rest,
 ):
-    edge_refs, corner_refs, rest = rest[:n_edge], rest[n_edge : 2 * n_edge], rest[2 * n_edge :]
-    out_ref, acts, slabs, weight, wide = rest
+    edge_refs, rest = rest[:n_edge], rest[n_edge:]
+    out_ref, token_ref, acts, slabs, weight, wide = rest
+    token_ref[...] = jnp.zeros_like(token_ref)
     t_n, r_n, w_n, c_n = lat_ref.shape
     h = lax.axis_index("height")
     mean, rstd = norm_ref[0:1], norm_ref[1:2]
@@ -331,8 +364,10 @@
     def act_of(f, r):
         if 0 <= r < r_n:
             return silu(past_ref[f, r] if f < 2 else lat_ref[f - 2, r])
-        refs = corner_refs if f < 2 else edge_refs
-        return silu((refs[0] if r < 0 else refs[-1])[f % 2])
+        which = 0 if r < 0 else n_edge - 1
+        if f < 2:
+            return silu(past_ref[f, r_n + which])
+        return silu(edge_refs[which][pl.ds((f - 2) * w_n, w_n), :])
 
     for f in range(t_n + 2):
         for r in range(-1, r_n + 1):
@@ -401,21 +436,26 @@
     gain, shift, offset = (v.reshape(1, c_n) for v in (group_norm_gain, group_norm_bias, kernel_bias))
     grid = (t_n, r_n, w_n, c_n)
     edge = (t_n, w_n, c_n)
+    small = shape((8, c_n), F32)
     rows = 27 * c_n
     unit = n_h * n_dp * 16
     total = -(-rows // unit) * unit
     share, piece = total // n_h, total // (n_h * n_dp)
 
-    grad, bias_part, *edge_list = call(
+    grad, bias_part, *corners = call(
         functools.partial(fold_body, n_edge),
-        [shape(grid, BF16), shape((8, c_n), F32)] + [shape(edge, BF16)] * n_edge,
+        [shape(grid, BF16), small] + [shape(edge, BF16)] * n_edge,
         cot,
         scratch=[pltpu.VMEM((2, 2 * w_n, c_n), F32)],
     )
-    (stats,) = call(stats_body, [shape((8, c_n), F32)], lat)
     halo = moved(grad, 1, 0)
+    corner_rows = facing(corners, 1)
+    stats, *edge_list = call(
+        functools.partial(stats_body, n_edge),
+        [small] + [shape((2 * t_n * w_n + TAB, c_n), BF16)] * n_edge,
+        lat, grad,
+    )
     edge_rows = facing(edge_list, 0)
-    corner_rows = facing(edge_list, 1)
 
     rounds = [("height", 1 << i) for i in range(n_h.bit_length() - 1)]
     rounds += [("tm", 1 << i) for i in range(n_t.bit_length() - 1)]
@@ -423,80 +463,73 @@
     other = None
     for axis, distance in rounds:
         if other is not None:
-            gap = stats[0:1] - other[0:1]
-            stats = jnp.concatenate(
-                [
-                    (stats[0:1] + other[0:1]) * 0.5,
-                    stats[1:2] + other[1:2] + gap * gap * (cells / 4),
-                    jnp.zeros((6, c_n), F32),
-                ]
-            )
-        other = swap(stats, axis, distance)
+            (stats,) = call(functools.partial(merge_body, cells), [small], stats, other)
+        if n_h == 2 and axis == "height":
+            other = edge_rows[0]
+        else:
+            other = swap(stats, axis, distance)
         cells = cells * 2
 
+    fold, dact, lead = call(
+        functools.partial(back_body, n_edge, n_h),
+        [shape((t_n * r_n * w_n, 9 * c_n), BF16), shape(grid, F32), shape((t_n, r_n + n_edge, w_n, c_n), BF16)],
+        lat, stats, grad, halo, kernel, *edge_rows, *corner_rows,
+        scratch=[pltpu.VMEM((3 * c_n, 9 * c_n), BF16)],
+        room=6 << 20,
+        flops=2 * 27 * t_n * r_n * w_n * c_n * c_n,
+    )
+    past = moved(lead, -1, 0)
     keep, table, dpre, norm, *sends = call(
-        functools.partial(main_body, n_edge, cells, n_h),
-        [shape((share, c_n), F32), shape((8, c_n), F32), shape(grid, F32), shape((8, c_n), F32)]
+        functools.partial(main_body, cells, n_h),
+        [shape((share, c_n), F32), small, shape(grid, F32), small]
         + [shape((share + TAB, c_n), BF16)] * (n_h - 1),
-        lat, stats, other, grad, halo, kernel, gain, shift, bias_part, *edge_rows, *corner_rows,
+        lat, stats, other, fold, dact, gain, shift, bias_part,
         scratch=[
             pltpu.VMEM((t_n * r_n * w_n, 3 * c_n), BF16),
-            pltpu.VMEM((t_n * r_n * w_n, 9 * c_n), BF16),
-            pltpu.VMEM((3 * c_n, 9 * c_n), BF16),
-            pltpu.VMEM((t_n * r_n * w_n, c_n), F32),
-            pltpu.VMEM((t_n * r_n * w_n, c_n), F32),
             pltpu.VMEM((total, c_n), F32),
         ],
-        flops=4 * 27 * t_n * r_n * w_n * c_n * c_n,
-    )
-
-    past = moved(lat, -1, 0)
-    if n_edge == 1:
-        row = jnp.where(lax.axis_index("height") == 0, r_n - 1, 0)
-        lat_edges = [lax.dynamic_index_in_dim(lat, row, 1, keepdims=False)]
-    else:
-        lat_edges = [lat[:, r_n - 1], lat[:, 0]]
-    lat_rows = facing(lat_edges, 0)
-    lat_corners = facing(lat_edges, -1)
+        room=8 << 20,
+        flops=2 * 27 * t_n * r_n * w_n * c_n * c_n,
+    )
 
     got = [swap(send, "height", s) for s, send in enumerate(sends, 1)]
     own, table, *sends = call(
         functools.partial(first_sum_body, n_h, n_dp),
-        [shape((piece, c_n), F32), shape((8, c_n), F32)] + [shape((piece + TAB, c_n), BF16)] * (n_dp - 1),
+        [shape((piece, c_n), F32), small] + [shape((piece + TAB, c_n), BF16)] * (n_dp - 1),
         keep, table, *got,
         scratch=[pltpu.VMEM((share, c_n), F32)],
     )
     got = [swap(send, "dp", s) for s, send in enumerate(sends, 1)]
-    (part,) = call(second_sum_body, [shape((piece + TAB, c_n), BF16)], own, table, *got)
+    upsampled, token = call(
+        functools.partial(forward_body, n_edge, n_h),
+        [shape(cot.shape, BF16), small],
+        lat, past, norm, kernel, gain, shift, offset, table, *edge_rows,
+        scratch=[
+            pltpu.VMEM((t_n + 2, r_n + 2, w_n, c_n), BF16),
+            pltpu.VMEM((t_n * r_n * w_n, 9 * c_n), BF16),
+            pltpu.VMEM((9 * c_n, 3 * c_n), BF16),
+            pltpu.VMEM((2, 2 * w_n, c_n), F32),
+        ],
+        room=6 << 20,
+        flops=2 * 27 * t_n * r_n * w_n * c_n * c_n,
+    )
+    (part,) = call(second_sum_body, [shape((piece + TAB, c_n), BF16)], own, table, token, *got)
     distance = 1
     while distance < n_t:
         other = swap(part, "tm", distance)
         distance *= 2
         if distance < n_t:
             (part,) = call(pair_sum_body, [shape((piece + TAB, c_n), BF16)], part, other)
-    part, table = call(last_sum_body, [shape((piece, c_n), BF16), shape((8, c_n), F32)], part, other)
+    part, table = call(last_sum_body, [shape((piece, c_n), BF16), small], part, other)
     got = [swap(part, "dp", s) for s in range(1, n_dp)]
-    (half,) = call(gather_body, [shape((share, c_n), BF16)], part, *got)
-    got = [swap(half, "height", s) for s in range(1, n_h)]
-    (kernel_grad,) = call(spread_body, [shape((rows, c_n), F32)], half, *got)
-
-    (upsampled,) = call(
-        functools.partial(forward_body, n_edge, n_h),
-        [shape(cot.shape, BF16)],
-        lat, past, norm, kernel, gain, shift, offset, *lat_rows, *lat_corners,
-        scratch=[
-            pltpu.VMEM((t_n + 2, r_n + 2, w_n, c_n), BF16),
-            pltpu.VMEM((t_n * r_n * w_n, 9 * c_n), BF16),
-            pltpu.VMEM((9 * c_n, 3 * c_n), BF16),
-            pltpu.VMEM((2, 2 * w_n, c_n), F32),
-        ],
-        flops=2 * 27 * t_n * r_n * w_n * c_n * c_n,
-    )
     latent_gradient, bias_grad, gain_grad, shift_grad = call(
         functools.partial(last_body, cells),
         [shape(grid, BF16)] + [shape((1, c_n), F32)] * 3,
         dpre, lat, norm, table, gain,
     )
+    (half,) = call(gather_body, [shape((share, c_n), BF16)], shift_grad, part, *got)
+    got = [swap(half, "height", s) for s in range(1, n_h)]
+    (kernel_grad,) = call(spread_body, [shape((rows, c_n), F32)], half, *got)
     return (
         upsampled[None],
         latent_gradient[None],

time: 100 us -> 65.9 us (0.66)
  Pallas kernels: 29.7 us -> 11.7 us
  waiting for transfers between devices: 37.1 us -> 24.5 us
  local copies, waits for them, and re-layouts: 5.75 us -> 3.01 us
    pallas_call x11 -> x14, Pallas kernels: 29.7 us -> 11.7 us  [call(): pl.pallas_call(body, out_shape=tuple(outs), in_specs=[VMEM] * len(args),...]
    ppermute x13 -> x12, waiting for transfers between devices: 30.2 us -> 19.1 us  [swap(): return lax.ppermute(block, axis, [(i, i ^ distance) for i in range(count)])]
    ppermute x4 -> x2, waiting for transfers between devices: 6.88 us -> 0.01 us  [across(): return lax.ppermute(block, ('tm', 'height'), route)]
    ppermute x2, waiting for transfers between devices: 0.01 us -> 5.42 us  [moved(): return lax.ppermute(block, ('tm', 'height'), route)]
    ppermute x13 -> x12, starting transfers between devices: 18.2 us -> 21 us  [swap(): return lax.ppermute(block, axis, [(i, i ^ distance) for i in range(count)])]
    unnamed x38 -> x16, local copies, waits for them, and re-layouts: 5.66 us -> 3.01 us
    ppermute x4 -> x2, starting transfers between devices: 3.71 us -> 1.83 us  [across(): return lax.ppermute(block, ('tm', 'height'), route)]
  transfers between devices with their start and end apart: 19 -> 16, of which waited for: 11 -> 9; matrix products, arithmetic and copies ran while one was open for 0% -> 0% of each run, Pallas kernels for 10% -> 11%
where the time goes in v2:
time: 65.9 us; the launch traced here: 65.6 us
  starting transfers between devices  25.6 us (39%)
  waiting for transfers between devices  24.5 us (37%)
  Pallas kernels  11.7 us (18%)
  local copies, waits for them, and re-layouts  3.01 us (5%)
  between operations  0.81 us (1%)
    ppermute x12, starting transfers between devices, swap(): return lax.ppermute(block, axis, [(i, i ^ distance) for i in range(count)])  21 us
    ppermute x12, waiting for transfers between devices, swap(): return lax.ppermute(block, axis, [(i, i ^ distance) for i in range(count)])  19.1 us
    pallas_call x14, Pallas kernels, call(): pl.pallas_call(body, out_shape=tuple(outs), in_specs=[VMEM] * len(args),...  11.7 us
    ppermute x2, waiting for transfers between devices, moved(): return lax.ppermute(block, ('tm', 'height'), route)  5.42 us
    unnamed x16, local copies, waits for them, and re-layouts  3.01 us
    ppermute x2, starting transfers between devices, moved(): return lax.ppermute(block, ('tm', 'height'), route)  2.75 us
    ppermute x2, starting transfers between devices, across(): return lax.ppermute(block, ('tm', 'height'), route)  1.83 us
  transfers between devices with their start and end apart: 16, of which 9 were waited for; matrix products, arithmetic and copies ran while one was open for 0% of the time, Pallas kernels for 11%

profile of v2, /device:TPU:0, one launch (start us, length us, event | category | flops | bytes accessed | tf_op | source)
XLA Modules:
  0.0 65.6 jit_solution(17412631350711631396)
XLA Ops:
  0.6 0.0 copy-start.1
  0.7 1.4 %copy-done.2 = bf16[1,2,8,320,128]{4,3,2,1,0:T(8,128)(2,1)S(1)} copy-done((bf16[1,2,8,320,128]{4,3,2,1,0:T(8,128)(2,1)S(1)}, bf16[1,2,8,320,128]{4,3,2,1,0:T(8,128)(2,1)}, u32[]{:S(2)}) %copy-start.2) | copy-done | bytes 1310744
  2.0 0.3 shard_map.109
  2.3 1.3 %collective-permute-start.2 = (bf16[2,4,160,128]{3,2,1,0:T(8,128)(2,1)S(1)}, bf16[2,4,160,128]{3,2,1,0:T(8,128)(2,1)S(1)}, u32[]{:S(2)}, u32[]{:S(2)}) collective-permute-start(bf16[2,4,160,128]{3,2,1,0:T(8,128)(2,1)S(1)} %get-tuple-element.32.grad_ref), channel_id=1, source_target_pairs={{2,0},{3,1},{4,2},{5,3},{6,4},{7,5},{10,8},{11,9},{12,10},{13,11},... | collective-permute-start | bytes 983048 | tf_op jit(solution)/shard_map/ppermute | solution.py:48
  3.6 0.0 copy-start
  3.6 1.0 %copy-done = bf16[1,2,4,160,128]{4,3,2,1,0:T(8,128)(2,1)S(1)} copy-done((bf16[1,2,4,160,128]{4,3,2,1,0:T(8,128)(2,1)S(1)}, bf16[1,2,4,160,128]{4,3,2,1,0:T(8,128)(2,1)}, u32[]{:S(2)}) %copy-start) | copy-done | bytes 327704
  4.6 0.2 shard_map.110
  4.7 0.6 collective-permute-start
  5.3 1.3 %collective-permute-start.3 = (bf16[2,160,128]{2,1,0:T(8,128)(2,1)S(1)}, bf16[2,160,128]{2,1,0:T(8,128)(2,1)S(1)}, u32[]{:S(2)}, u32[]{:S(2)}) collective-permute-start(bf16[2,160,128]{2,1,0:T(8,128)(2,1)S(1)} %get-tuple-element.35), channel_id=1, source_target_pairs={{3,0},{2,1},{5,2},{4,3},{7,4},{6,5},{11,8},{10,9},{13,10},{12,11},... | collective-permute-start | bytes 245768 | tf_op jit(solution)/shard_map/ppermute | solution.py:58
  6.6 3.9 %collective-permute-start.1 = (f32[8,128]{1,0:T(8,128)S(1)}, f32[8,128]{1,0:T(8,128)S(1)}, u32[]{:S(2)}, u32[]{:S(2)}) collective-permute-start(f32[8,128]{1,0:T(8,128)S(1)} %shard_map.111.a_ref), channel_id=1, source_target_pairs={{0,2},{2,0},{4,6},{6,4},{1,3},{3,1},{5,7},{7,5},{8,10},{10,8},{12,... | collective-permute-start | bytes 12296 | tf_op jit(solution)/shard_map/ppermute | solution.py:38
  10.5 6.3 %collective-permute-done.1.b_ref = f32[8,128]{1,0:T(8,128)S(1)} collective-permute-done((f32[8,128]{1,0:T(8,128)S(1)}, f32[8,128]{1,0:T(8,128)S(1)}, u32[]{:S(2)}, u32[]{:S(2)}) %collective-permute-start.1) | collective-permute-done | bytes 4128 | tf_op jit(solution)/shard_map/ppermute | solution.py:38
  16.8 0.0 copy-start.3
  16.8 0.0 copy-start.6
  16.8 2.9 %collective-permute-start.5 = (f32[8,128]{1,0:T(8,128)S(1)}, f32[8,128]{1,0:T(8,128)S(1)}, u32[]{:S(2)}, u32[]{:S(2)}) collective-permute-start(f32[8,128]{1,0:T(8,128)S(1)} %shard_map.112.stats_ref.mine_ref), channel_id=1, source_target_pairs={{0,4},{2,6},{4,0},{6,2},{1,5},{3,7},{5,1},{7,3},{8,12},{10,14},{12... | collective-permute-start | bytes 12296 | tf_op jit(solution)/shard_map/ppermute | solution.py:38
  19.7 0.0 collective-permute-done.3.rest_1_
  19.7 0.0 collective-permute-done.2.halo_ref
  19.7 2.1 %shard_map.113 = (bf16[1280,1152]{1,0:T(8,128)(2,1)S(1)}, f32[2,4,160,128]{3,2,1,0:T(8,128)S(1)}, bf16[2,5,160,128]{3,2,1,0:T(8,128)(2,1)S(1)}) custom-call(bf16[2,4,160,128]{3,2,1,0:T(8,128)(2,1)S(1)} %bitcast.12, f32[8,128]{1,0:T(8,128)S(1)} %shard_map.112.stats_ref.mine_ref, bf16[2,4,160,128]{3,2,1,0:T(8,128)(2,1)S(1)} %get-tuple-element.32.grad_ref, ...), custom_call_target="tpu_custom_call" | custom-call | flops 1132462080 | bytes 6139904 | tf_op jit(solution)/shard_map/pallas_call | solution.py:21
  21.8 0.0 collective-permute-done.5.other_ref
  21.9 0.0 copy-start.7
  21.9 2.7 %shard_map.114 = (f32[1728,128]{1,0:T(8,128)S(1)}, f32[8,128]{1,0:T(8,128)S(1)}, f32[2,4,160,128]{3,2,1,0:T(8,128)S(1)}, f32[8,128]{1,0:T(8,128)S(1)}, bf16[1760,128]{1,0:T(8,128)(2,1)S(1)}) custom-call(bf16[2,4,160,128]{3,2,1,0:T(8,128)(2,1)S(1)} %bitcast.13, f32[8,128]{1,0:T(8,128)S(1)} %shard_map.112.stats_ref.mine_ref, ...), custom_call_target="tpu_custom_call" | custom-call | flops 1132462080 | bytes 5944320 | tf_op jit(solution)/shard_map/pallas_call | solution.py:21
  24.6 0.1 collective-permute-start.6
  24.7 1.5 %collective-permute-start.4 = (bf16[2,5,160,128]{3,2,1,0:T(8,128)(2,1)S(1)}, bf16[2,5,160,128]{3,2,1,0:T(8,128)(2,1)S(1)}, u32[]{:S(2)}, u32[]{:S(2)}) collective-permute-start(bf16[2,5,160,128]{3,2,1,0:T(8,128)(2,1)S(1)} %get-tuple-element.36), channel_id=1, source_target_pairs={{0,2},{1,3},{2,4},{3,5},{4,6},{5,7},{8,10},{9,11},{10,12},{11,13},... | collective-permute-start | bytes 1228808 | tf_op jit(solution)/shard_map/ppermute | solution.py:48
  26.1 0.3 collective-permute-done.6.rest_0_
  26.5 0.2 shard_map.115
  26.6 1.5 %collective-permute-start.7 = (bf16[464,128]{1,0:T(8,128)(2,1)S(1)}, bf16[464,128]{1,0:T(8,128)(2,1)S(1)}, u32[]{:S(2)}, u32[]{:S(2)}) collective-permute-start(bf16[464,128]{1,0:T(8,128)(2,1)S(1)} %get-tuple-element.49), channel_id=1, source_target_pairs={{0,8},{8,0},{16,24},{24,16},{1,9},{9,1},{17,25},{25,17},{2,10},{10... | collective-permute-start | bytes 356360 | tf_op jit(solution)/shard_map/ppermute | solution.py:38
  28.2 1.5 %collective-permute-start.8 = (bf16[464,128]{1,0:T(8,128)(2,1)S(1)}, bf16[464,128]{1,0:T(8,128)(2,1)S(1)}, u32[]{:S(2)}, u32[]{:S(2)}) collective-permute-start(bf16[464,128]{1,0:T(8,128)(2,1)S(1)} %get-tuple-element.50), channel_id=1, source_target_pairs={{0,16},{8,24},{16,0},{24,8},{1,17},{9,25},{17,1},{25,9},{2,18},{10... | collective-permute-start | bytes 356360 | tf_op jit(solution)/shard_map/ppermute | solution.py:38
  29.7 0.5 collective-permute-start.9
  30.2 5.4 %collective-permute-done.4.past_ref = bf16[2,5,160,128]{3,2,1,0:T(8,128)(2,1)S(1)} collective-permute-done((bf16[2,5,160,128]{3,2,1,0:T(8,128)(2,1)S(1)}, bf16[2,5,160,128]{3,2,1,0:T(8,128)(2,1)S(1)}, u32[]{:S(2)}, u32[]{:S(2)}) %collective-permute-start.4) | collective-permute-done | bytes 409632 | tf_op jit(solution)/shard_map/ppermute | solution.py:48
  35.6 3.7 %shard_map.116 = (bf16[2,8,320,128]{3,2,1,0:T(8,128)(2,1)}, f32[8,128]{1,0:T(8,128)S(1)}) custom-call(bf16[2,4,160,128]{3,2,1,0:T(8,128)(2,1)S(1)} %bitcast.14, bf16[2,5,160,128]{3,2,1,0:T(8,128)(2,1)S(1)} %collective-permute-done.4.past_ref, f32[8,128]{1,0:T(8,128)S(1)} %get-tuple-element.40.norm_ref, bf16[3,3,384,128]{3,2,1,0:T(8,128)(2,1)S(1)} %copy-done.5, ...), custom_call_target="tpu_custom_call" | custom-call | flops 1132462080 | bytes 3118592 | tf_op jit(solution)/shard_map/pallas_call | solution.py:21
  39.3 0.0 collective-permute-done.7.rest_0_
  39.3 0.0 collective-permute-done.8.rest_1_
  39.3 0.0 collective-permute-done.9.rest_2_
  39.3 0.1 shard_map.117.a_ref
  39.4 3.2 %collective-permute-start.10 = (bf16[464,128]{1,0:T(8,128)(2,1)S(1)}, bf16[464,128]{1,0:T(8,128)(2,1)S(1)}, u32[]{:S(2)}, u32[]{:S(2)}) collective-permute-start(bf16[464,128]{1,0:T(8,128)(2,1)S(1)} %shard_map.117.a_ref), channel_id=1, source_target_pairs={{0,2},{2,0},{4,6},{6,4},{1,3},{3,1},{5,7},{7,5},{8,10},{10,8},{12,... | collective-permute-start | bytes 356360 | tf_op jit(solution)/shard_map/ppermute | solution.py:38
  42.6 3.0 %collective-permute-done.10.b_ref = bf16[464,128]{1,0:T(8,128)(2,1)S(1)} collective-permute-done((bf16[464,128]{1,0:T(8,128)(2,1)S(1)}, bf16[464,128]{1,0:T(8,128)(2,1)S(1)}, u32[]{:S(2)}, u32[]{:S(2)}) %collective-permute-start.10) | collective-permute-done | bytes 118816 | tf_op jit(solution)/shard_map/ppermute | solution.py:38
  45.7 3.8 %collective-permute-start.11 = (bf16[464,128]{1,0:T(8,128)(2,1)S(1)}, bf16[464,128]{1,0:T(8,128)(2,1)S(1)}, u32[]{:S(2)}, u32[]{:S(2)}) collective-permute-start(bf16[464,128]{1,0:T(8,128)(2,1)S(1)} %shard_map.118.a_ref), channel_id=1, source_target_pairs={{0,4},{2,6},{4,0},{6,2},{1,5},{3,7},{5,1},{7,3},{8,12},{10,14},{12... | collective-permute-start | bytes 356360 | tf_op jit(solution)/shard_map/ppermute | solution.py:38
  49.5 4.4 %collective-permute-done.11.b_ref = bf16[464,128]{1,0:T(8,128)(2,1)S(1)} collective-permute-done((bf16[464,128]{1,0:T(8,128)(2,1)S(1)}, bf16[464,128]{1,0:T(8,128)(2,1)S(1)}, u32[]{:S(2)}, u32[]{:S(2)}) %collective-permute-start.11) | collective-permute-done | bytes 118816 | tf_op jit(solution)/shard_map/ppermute | solution.py:38
  53.9 2.5 %collective-permute-start.14 = (bf16[432,128]{1,0:T(8,128)(2,1)S(1)}, bf16[432,128]{1,0:T(8,128)(2,1)S(1)}, u32[]{:S(2)}, u32[]{:S(2)}) collective-permute-start(bf16[432,128]{1,0:T(8,128)(2,1)S(1)} %get-tuple-element.55.own_ref), channel_id=1, source_target_pairs={{0,24},{8,16},{16,8},{24,0},{1,25},{9,17},{17,9},{25,1},{2,26},{10... | collective-permute-start | bytes 331784 | tf_op jit(solution)/shard_map/ppermute | solution.py:38
  56.4 0.5 collective-permute-start.13
  57.0 0.5 collective-permute-start.12
  57.5 1.0 %shard_map.120 = (bf16[2,4,160,128]{3,2,1,0:T(8,128)(2,1)}, f32[1,128]{1,0:T(1,128)}, f32[1,128]{1,0:T(1,128)}, f32[1,128]{1,0:T(1,128)}) custom-call(f32[2,4,160,128]{3,2,1,0:T(8,128)S(1)} %get-tuple-element.46.dpre_ref, bf16[2,4,160,128]{3,2,1,0:T(8,128)(2,1)S(1)} %bitcast.15, f32[8,128]{1,0:T(8,128)S(1)} %get-tuple-element.40.norm_ref, ...), custom_call_target="tpu_custom_call" | custom-call | flops 1000000 | bytes 1320960 | tf_op jit(solution)/shard_map/pallas_call | solution.py:21
  58.5 1.7 %collective-permute-done.14.rest_2_ = bf16[432,128]{1,0:T(8,128)(2,1)S(1)} collective-permute-done((bf16[432,128]{1,0:T(8,128)(2,1)S(1)}, bf16[432,128]{1,0:T(8,128)(2,1)S(1)}, u32[]{:S(2)}, u32[]{:S(2)}) %collective-permute-start.14) | collective-permute-done | bytes 110624 | tf_op jit(solution)/shard_map/ppermute | solution.py:38
  60.2 1.3 %collective-permute-done.13.rest_1_ = bf16[432,128]{1,0:T(8,128)(2,1)S(1)} collective-permute-done((bf16[432,128]{1,0:T(8,128)(2,1)S(1)}, bf16[432,128]{1,0:T(8,128)(2,1)S(1)}, u32[]{:S(2)}, u32[]{:S(2)}) %collective-permute-start.13) | collective-permute-done | bytes 110624 | tf_op jit(solution)/shard_map/ppermute | solution.py:38
  61.5 0.2 collective-permute-done.12.rest_0_
  61.7 0.7 copy-done.4
  62.4 0.1 collective-permute-start.15
  62.5 1.8 %collective-permute-done.15.rest_0_ = bf16[1728,128]{1,0:T(8,128)(2,1)S(1)} collective-permute-done((bf16[1728,128]{1,0:T(8,128)(2,1)S(1)}, bf16[1728,128]{1,0:T(8,128)(2,1)S(1)}, u32[]{:S(2)}, u32[]{:S(2)}) %collective-permute-start.15) | collective-permute-done | bytes 442400 | tf_op jit(solution)/shard_map/ppermute | solution.py:38
  64.3 1.3 %shard_map.122 = f32[3456,128]{1,0:T(8,128)} custom-call(bf16[1728,128]{1,0:T(8,128)(2,1)S(1)} %shard_map.121.own_ref, bf16[1728,128]{1,0:T(8,128)(2,1)S(1)} %collective-permute-done.15.rest_0_), custom_call_target="tpu_custom_call" | custom-call | flops 1000000 | bytes 2654208 | tf_op jit(solution)/shard_map/pallas_call | solution.py:21
  (14 shorter events, 0.2 us)
Async XLA Ops:
  0.6 19.1 %copy-start.1 = (bf16[1,2,4,160,128]{4,3,2,1,0:T(8,128)(2,1)S(1)}, bf16[1,2,4,160,128]{4,3,2,1,0:T(8,128)(2,1)}, u32[]{:S(2)}) copy-start(bf16[1,2,4,160,128]{4,3,2,1,0:T(8,128)(2,1)} %param.6) | copy-start | bytes 983044
  0.6 1.4 %copy-start.2 = (bf16[1,2,8,320,128]{4,3,2,1,0:T(8,128)(2,1)S(1)}, bf16[1,2,8,320,128]{4,3,2,1,0:T(8,128)(2,1)}, u32[]{:S(2)}) copy-start(bf16[1,2,8,320,128]{4,3,2,1,0:T(8,128)(2,1)} %param.7) | copy-start | bytes 3932164
  2.0 17.7 %copy-start.5 = (bf16[3,3,384,128]{3,2,1,0:T(8,128)(2,1)S(1)}, bf16[3,3,384,128]{3,2,1,0:T(8,128)(2,1)}, u32[]{:S(2)}) copy-start(bf16[3,3,384,128]{3,2,1,0:T(8,128)(2,1)} %kernel_ref.3) | copy-start | bytes 2654212
  2.3 17.4 %collective-permute-start.2 = (bf16[2,4,160,128]{3,2,1,0:T(8,128)(2,1)S(1)}, bf16[2,4,160,128]{3,2,1,0:T(8,128)(2,1)S(1)}, u32[]{:S(2)}, u32[]{:S(2)}) collective-permute-start(bf16[2,4,160,128]{3,2,1,0:T(8,128)(2,1)S(1)} %get-tuple-element.32.grad_ref), channel_id=1, source_target_pairs={{2,0},{3,1},{4,2},{5,3},{6,4},{7,5},{10,8},{11,9},{12,10},{13,11},... | collective-permute-start | bytes 983048 | tf_op jit(solution)/shard_map/ppermute | solution.py:48
  3.6 1.0 %copy-start = (bf16[1,2,4,160,128]{4,3,2,1,0:T(8,128)(2,1)S(1)}, bf16[1,2,4,160,128]{4,3,2,1,0:T(8,128)(2,1)}, u32[]{:S(2)}) copy-start(bf16[1,2,4,160,128]{4,3,2,1,0:T(8,128)(2,1)} %param.6) | copy-start | bytes 983044
  4.7 1.8 %collective-permute-start = (bf16[672,128]{1,0:T(8,128)(2,1)S(1)}, bf16[672,128]{1,0:T(8,128)(2,1)S(1)}, u32[]{:S(2)}, u32[]{:S(2)}) collective-permute-start(bf16[672,128]{1,0:T(8,128)(2,1)S(1)} %get-tuple-element.34), channel_id=1, source_target_pairs={{1,0},{0,1},{3,2},{2,3},{5,4},{4,5},{7,6},{6,7},{9,8},{8,9},{11,10... | collective-permute-start | bytes 516104 | tf_op jit(solution)/shard_map/ppermute | solution.py:58
  5.3 14.4 %collective-permute-start.3 = (bf16[2,160,128]{2,1,0:T(8,128)(2,1)S(1)}, bf16[2,160,128]{2,1,0:T(8,128)(2,1)S(1)}, u32[]{:S(2)}, u32[]{:S(2)}) collective-permute-start(bf16[2,160,128]{2,1,0:T(8,128)(2,1)S(1)} %get-tuple-element.35), channel_id=1, source_target_pairs={{3,0},{2,1},{5,2},{4,3},{7,4},{6,5},{11,8},{10,9},{13,10},{12,11},... | collective-permute-start | bytes 245768 | tf_op jit(solution)/shard_map/ppermute | solution.py:58
  6.6 10.2 %collective-permute-start.1 = (f32[8,128]{1,0:T(8,128)S(1)}, f32[8,128]{1,0:T(8,128)S(1)}, u32[]{:S(2)}, u32[]{:S(2)}) collective-permute-start(f32[8,128]{1,0:T(8,128)S(1)} %shard_map.111.a_ref), channel_id=1, source_target_pairs={{0,2},{2,0},{4,6},{6,4},{1,3},{3,1},{5,7},{7,5},{8,10},{10,8},{12,... | collective-permute-start | bytes 12296 | tf_op jit(solution)/shard_map/ppermute | solution.py:38
  16.8 5.0 %copy-start.3 = (f32[128]{0:T(128)S(1)}, f32[128]{0:T(128)}, u32[]{:S(2)}) copy-start(f32[128]{0:T(128)} %param.8) | copy-start | bytes 1540
  16.8 5.0 %copy-start.6 = (f32[128]{0:T(128)S(1)}, f32[128]{0:T(128)}, u32[]{:S(2)}) copy-start(f32[128]{0:T(128)} %param.9) | copy-start | bytes 1540
  16.8 5.0 %collective-permute-start.5 = (f32[8,128]{1,0:T(8,128)S(1)}, f32[8,128]{1,0:T(8,128)S(1)}, u32[]{:S(2)}, u32[]{:S(2)}) collective-permute-start(f32[8,128]{1,0:T(8,128)S(1)} %shard_map.112.stats_ref.mine_ref), channel_id=1, source_target_pairs={{0,4},{2,6},{4,0},{6,2},{1,5},{3,7},{5,1},{7,3},{8,12},{10,14},{12... | collective-permute-start | bytes 12296 | tf_op jit(solution)/shard_map/ppermute | solution.py:38
  21.9 13.8 %copy-start.7 = (f32[128]{0:T(128)S(1)}, f32[128]{0:T(128)}, u32[]{:S(2)}) copy-start(f32[128]{0:T(128)} %param.11) | copy-start | bytes 1540
  24.6 1.9 %collective-permute-start.6 = (bf16[1760,128]{1,0:T(8,128)(2,1)S(1)}, bf16[1760,128]{1,0:T(8,128)(2,1)S(1)}, u32[]{:S(2)}, u32[]{:S(2)}) collective-permute-start(bf16[1760,128]{1,0:T(8,128)(2,1)S(1)} %get-tuple-element.43), channel_id=1, source_target_pairs={{0,1},{1,0},{2,3},{3,2},{4,5},{5,4},{6,7},{7,6},{8,9},{9,8},{10,11... | collective-permute-start | bytes 1351688 | tf_op jit(solution)/shard_map/ppermute | solution.py:38
  24.7 10.9 %collective-permute-start.4 = (bf16[2,5,160,128]{3,2,1,0:T(8,128)(2,1)S(1)}, bf16[2,5,160,128]{3,2,1,0:T(8,128)(2,1)S(1)}, u32[]{:S(2)}, u32[]{:S(2)}) collective-permute-start(bf16[2,5,160,128]{3,2,1,0:T(8,128)(2,1)S(1)} %get-tuple-element.36), channel_id=1, source_target_pairs={{0,2},{1,3},{2,4},{3,5},{4,6},{5,7},{8,10},{9,11},{10,12},{11,13},... | collective-permute-start | bytes 1228808 | tf_op jit(solution)/shard_map/ppermute | solution.py:48
  26.6 12.7 %collective-permute-start.7 = (bf16[464,128]{1,0:T(8,128)(2,1)S(1)}, bf16[464,128]{1,0:T(8,128)(2,1)S(1)}, u32[]{:S(2)}, u32[]{:S(2)}) collective-permute-start(bf16[464,128]{1,0:T(8,128)(2,1)S(1)} %get-tuple-element.49), channel_id=1, source_target_pairs={{0,8},{8,0},{16,24},{24,16},{1,9},{9,1},{17,25},{25,17},{2,10},{10... | collective-permute-start | bytes 356360 | tf_op jit(solution)/shard_map/ppermute | solution.py:38
  28.2 11.1 %collective-permute-start.8 = (bf16[464,128]{1,0:T(8,128)(2,1)S(1)}, bf16[464,128]{1,0:T(8,128)(2,1)S(1)}, u32[]{:S(2)}, u32[]{:S(2)}) collective-permute-start(bf16[464,128]{1,0:T(8,128)(2,1)S(1)} %get-tuple-element.50), channel_id=1, source_target_pairs={{0,16},{8,24},{16,0},{24,8},{1,17},{9,25},{17,1},{25,9},{2,18},{10... | collective-permute-start | bytes 356360 | tf_op jit(solution)/shard_map/ppermute | solution.py:38
  29.7 9.6 %collective-permute-start.9 = (bf16[464,128]{1,0:T(8,128)(2,1)S(1)}, bf16[464,128]{1,0:T(8,128)(2,1)S(1)}, u32[]{:S(2)}, u32[]{:S(2)}) collective-permute-start(bf16[464,128]{1,0:T(8,128)(2,1)S(1)} %get-tuple-element.51), channel_id=1, source_target_pairs={{0,24},{8,16},{16,8},{24,0},{1,25},{9,17},{17,9},{25,1},{2,26},{10... | collective-permute-start | bytes 356360 | tf_op jit(solution)/shard_map/ppermute | solution.py:38
  39.4 6.3 %collective-permute-start.10 = (bf16[464,128]{1,0:T(8,128)(2,1)S(1)}, bf16[464,128]{1,0:T(8,128)(2,1)S(1)}, u32[]{:S(2)}, u32[]{:S(2)}) collective-permute-start(bf16[464,128]{1,0:T(8,128)(2,1)S(1)} %shard_map.117.a_ref), channel_id=1, source_target_pairs={{0,2},{2,0},{4,6},{6,4},{1,3},{3,1},{5,7},{7,5},{8,10},{10,8},{12,... | collective-permute-start | bytes 356360 | tf_op jit(solution)/shard_map/ppermute | solution.py:38
  45.7 8.2 %collective-permute-start.11 = (bf16[464,128]{1,0:T(8,128)(2,1)S(1)}, bf16[464,128]{1,0:T(8,128)(2,1)S(1)}, u32[]{:S(2)}, u32[]{:S(2)}) collective-permute-start(bf16[464,128]{1,0:T(8,128)(2,1)S(1)} %shard_map.118.a_ref), channel_id=1, source_target_pairs={{0,4},{2,6},{4,0},{6,2},{1,5},{3,7},{5,1},{7,3},{8,12},{10,14},{12... | collective-permute-start | bytes 356360 | tf_op jit(solution)/shard_map/ppermute | solution.py:38
  53.9 6.3 %collective-permute-start.14 = (bf16[432,128]{1,0:T(8,128)(2,1)S(1)}, bf16[432,128]{1,0:T(8,128)(2,1)S(1)}, u32[]{:S(2)}, u32[]{:S(2)}) collective-permute-start(bf16[432,128]{1,0:T(8,128)(2,1)S(1)} %get-tuple-element.55.own_ref), channel_id=1, source_target_pairs={{0,24},{8,16},{16,8},{24,0},{1,25},{9,17},{17,9},{25,1},{2,26},{10... | collective-permute-start | bytes 331784 | tf_op jit(solution)/shard_map/ppermute | solution.py:38
  56.4 5.0 %collective-permute-start.13 = (bf16[432,128]{1,0:T(8,128)(2,1)S(1)}, bf16[432,128]{1,0:T(8,128)(2,1)S(1)}, u32[]{:S(2)}, u32[]{:S(2)}) collective-permute-start(bf16[432,128]{1,0:T(8,128)(2,1)S(1)} %get-tuple-element.55.own_ref), channel_id=1, source_target_pairs={{0,16},{8,24},{16,0},{24,8},{1,17},{9,25},{17,1},{25,9},{2,18},{10... | collective-permute-start | bytes 331784 | tf_op jit(solution)/shard_map/ppermute | solution.py:38
  57.0 4.8 %collective-permute-start.12 = (bf16[432,128]{1,0:T(8,128)(2,1)S(1)}, bf16[432,128]{1,0:T(8,128)(2,1)S(1)}, u32[]{:S(2)}, u32[]{:S(2)}) collective-permute-start(bf16[432,128]{1,0:T(8,128)(2,1)S(1)} %get-tuple-element.55.own_ref), channel_id=1, source_target_pairs={{0,8},{8,0},{16,24},{24,16},{1,9},{9,1},{17,25},{25,17},{2,10},{10... | collective-permute-start | bytes 331784 | tf_op jit(solution)/shard_map/ppermute | solution.py:38
  61.7 0.7 copy-start.4
  62.4 1.9 %collective-permute-start.15 = (bf16[1728,128]{1,0:T(8,128)(2,1)S(1)}, bf16[1728,128]{1,0:T(8,128)(2,1)S(1)}, u32[]{:S(2)}, u32[]{:S(2)}) collective-permute-start(bf16[1728,128]{1,0:T(8,128)(2,1)S(1)} %shard_map.121.own_ref), channel_id=1, source_target_pairs={{0,1},{1,0},{2,3},{3,2},{4,5},{5,4},{6,7},{7,6},{8,9},{9,8},{10,11... | collective-permute-start | bytes 1327112 | tf_op jit(solution)/shard_map/ppermute | solution.py:38

commit v3 on v2

--- a/solution.py
+++ b/solution.py
@@ -8,6 +8,7 @@
 from jax.experimental.pallas import tpu as pltpu
 from jax.sharding import PartitionSpec as P
 
+
 GROUPS = 32
 F32 = jnp.float32
 BF16 = jnp.bfloat16
@@ -15,17 +16,23 @@
 VMEM = pl.BlockSpec(memory_space=pltpu.VMEM)
 
 
-def call(body, outs, *args, scratch=(), flops=1_000_000, room=2 << 20):
-    moved = sum(a.size * a.dtype.itemsize for a in (*args, *outs))
-    held = sum(math.prod(s.shape) * jnp.dtype(s.dtype).itemsize for s in scratch)
+HBM = pl.BlockSpec(memory_space=pltpu.HBM)
+
+
+def call(body, outs, *args, scratch=(), flops=1_000_000, room=2 << 20, far=(), far_out=(), alias=None):
+    size = [a.size * a.dtype.itemsize for a in (*args, *outs)]
+    out_of = {*far, *(len(args) + i for i in far_out)}
+    near = sum(n for i, n in enumerate(size) if i not in out_of)
+    held = sum(math.prod(s.shape) * jnp.dtype(s.dtype).itemsize for s in scratch if s.memory_space == pltpu.VMEM)
     return pl.pallas_call(
         body,
         out_shape=tuple(outs),
-        in_specs=[VMEM] * len(args),
-        out_specs=tuple([VMEM] * len(outs)),
+        in_specs=[HBM if i in far else VMEM for i in range(len(args))],
+        out_specs=tuple(HBM if i in far_out else VMEM for i in range(len(outs))),
         scratch_shapes=list(scratch),
-        compiler_params=pltpu.CompilerParams(vmem_limit_bytes=moved + held + room),
-        cost_estimate=pl.CostEstimate(flops=flops, bytes_accessed=moved, transcendentals=0),
+        input_output_aliases=alias or {},
+        compiler_params=pltpu.CompilerParams(vmem_limit_bytes=near + held + room),
+        cost_estimate=pl.CostEstimate(flops=flops, bytes_accessed=sum(size), transcendentals=0),
     )(*args)
 
 
@@ -101,33 +108,40 @@
     return jnp.where(row == x.shape[0] - 1, x if edge else 0.0, pltpu.roll(x, x.shape[0] - 1, 0))
 
 
-def fold_body(edge_n, cot_ref, out_ref, bias_ref, *rest):
-    edge_refs, wide = rest[:edge_n], rest[edge_n]
-    t_n, r2, w2, c_n = cot_ref.shape
-    r_n, w_n = r2 // 2, w2 // 2
-    total = jnp.zeros((8, c_n), F32)
-    for t in range(t_n):
-        for r in range(r_n):
-            slot = (t * r_n + r) % 2
-            wide[slot] = cot_ref[t, 2 * r].astype(F32) + cot_ref[t, 2 * r + 1].astype(F32)
-            value = wide[slot, pl.ds(0, w_n, stride=2), :] + wide[slot, pl.ds(1, w_n, stride=2), :]
-            total += jnp.sum(value.reshape(w_n // 8, 8, c_n), axis=0)
-            out_ref[t, r] = value.astype(BF16)
-    bias_ref[...] = jnp.broadcast_to(jnp.sum(total, axis=0, keepdims=True), (8, c_n))
-    for ref, row in zip(edge_refs, facing_rows(edge_n, r_n)):
-        ref[...] = out_ref[:, row]
-
-
 def facing_rows(edge_n, r_n):
     if edge_n == 1:
         return [jnp.where(lax.axis_index("height") == 0, r_n - 1, 0)]
     return [r_n - 1, 0]
 
 
-def stats_body(edge_n, lat_ref, grad_ref, out_ref, *edge_refs):
+def front_body(edge_n, cot_hbm, lat_hbm, lat_ref, grad_ref, bias_ref, stats_ref, *rest):
+    edge_refs, corner_refs, (cot_ref, wide, cot_sem, lat_sem) = rest[:edge_n], rest[edge_n : 2 * edge_n], rest[2 * edge_n :]
     t_n, r_n, w_n, c_n = lat_ref.shape
+    cot_copies = [
+        pltpu.make_async_copy(
+            cot_hbm.at[t, pl.ds(2 * r, 2)], cot_ref.at[t, pl.ds(2 * r, 2)], cot_sem.at[t * r_n + r]
+        )
+        for t in range(t_n)
+        for r in range(r_n)
+    ]
+    lat_copies = [pltpu.make_async_copy(lat_hbm.at[t], lat_ref.at[t], lat_sem.at[t]) for t in range(t_n)]
+    for copy in (*cot_copies, *lat_copies):
+        copy.start()
+
     total = jnp.zeros((8, c_n), F32)
     for t in range(t_n):
+        for r in range(r_n):
+            slot = (t * r_n + r) % 2
+            cot_copies[t * r_n + r].wait()
+            wide[slot] = cot_ref[t, 2 * r].astype(F32) + cot_ref[t, 2 * r + 1].astype(F32)
+            value = wide[slot, pl.ds(0, w_n, stride=2), :] + wide[slot, pl.ds(1, w_n, stride=2), :]
+            total += jnp.sum(value.reshape(w_n // 8, 8, c_n), axis=0)
+            grad_ref[t, r] = value.astype(BF16)
+    bias_ref[...] = jnp.broadcast_to(jnp.sum(total, axis=0, keepdims=True), (8, c_n))
+
+    total = jnp.zeros((8, c_n), F32)
+    for t in range(t_n):
+        lat_copies[t].wait()
         for r in range(r_n):
             total += jnp.sum(lat_ref[t, r].astype(F32).reshape(w_n // 8, 8, c_n), axis=0)
     mean = jnp.sum(total, axis=0, keepdims=True) / (t_n * r_n * w_n)
@@ -139,12 +153,13 @@
     square = jnp.sum(square, axis=0, keepdims=True)
     row = lax.broadcasted_iota(jnp.int32, (8, c_n), 0)
     stats = jnp.where(row == 0, mean, jnp.where(row == 1, square, 0.0))
-    out_ref[...] = stats
-    for ref, row in zip(edge_refs, facing_rows(edge_n, r_n)):
+    stats_ref[...] = stats
+    for edge_ref, corner_ref, row in zip(edge_refs, corner_refs, facing_rows(edge_n, r_n)):
+        corner_ref[...] = grad_ref[:, row]
         for t in range(t_n):
-            ref[pl.ds(t * w_n, w_n), :] = lat_ref[t, row]
-            ref[pl.ds((t_n + t) * w_n, w_n), :] = grad_ref[t, row]
-        ref[pl.ds(2 * t_n * w_n, TAB), :] = packed(stats)
+            edge_ref[pl.ds(t * w_n, w_n), :] = lat_ref[t, row]
+            edge_ref[pl.ds((t_n + t) * w_n, w_n), :] = grad_ref[t, row]
+        edge_ref[pl.ds(2 * t_n * w_n, TAB), :] = packed(stats)
 
 
 def merged(a, b, cells):
@@ -164,20 +179,24 @@
     out_ref[...] = jnp.where(row == 0, mean, jnp.where(row == 1, square, 0.0))
 
 
-def back_body(n_edge, n_h, lat_ref, stats_ref, grad_ref, halo_ref, kernel_ref, *rest):
+def lead_body(lat_ref, *rest):
+    edge_refs, lead_ref = rest[:-1], rest[-1]
+    t_n, r_n, w_n, _ = lat_ref.shape
+    for t in range(t_n):
+        for r in range(r_n):
+            lead_ref[t, r] = lat_ref[t, r]
+        for e, ref in enumerate(edge_refs):
+            lead_ref[t, r_n + e] = ref[pl.ds(t * w_n, w_n), :]
+
+
+def back_body(n_edge, n_h, grad_ref, halo_ref, kernel_ref, *rest):
     edge_refs, corner_refs, rest = rest[:n_edge], rest[n_edge : 2 * n_edge], rest[2 * n_edge :]
-    fold, dact_ref, lead_ref, weight = rest
-    t_n, r_n, w_n, c_n = lat_ref.shape
+    fold, dact_ref, weight = rest
+    t_n, r_n, w_n, c_n = grad_ref.shape
     h = lax.axis_index("height")
     top = (h == 0).astype(F32)
     bottom = (h == n_h - 1).astype(F32)
     first = (lax.axis_index("tm") == 0).astype(F32)
-
-    for t in range(t_n):
-        for r in range(r_n):
-            lead_ref[t, r] = lat_ref[t, r]
-        for e, ref in enumerate(edge_refs):
-            lead_ref[t, r_n + e] = ref[pl.ds(t * w_n, w_n), :]
 
     def source(f, r):
         if 0 <= r < r_n:
@@ -225,15 +244,23 @@
 
 
 def main_body(
-    cells, n_h,
-    lat_ref, mine_ref, other_ref, fold_ref, dact_ref, gain_ref, shift_ref, bias_ref, *rest,
+    cells, n_h, n_t,
+    lat_ref, fold_ref, dact_ref, gain_ref, shift_ref, bias_ref, *rest,
 ):
+    stats_refs, rest = rest[:n_t], rest[n_t:]
     keep_ref, table_ref, dpre_ref, norm_ref = rest[:4]
     send_refs, (acts, sums) = rest[4 : 3 + n_h], rest[3 + n_h :]
     t_n, r_n, w_n, c_n = lat_ref.shape
     h = lax.axis_index("height")
 
-    channel_mean, square = merged(mine_ref[...], other_ref[...], cells)
+    parts = [ref[...] for ref in stats_refs]
+    of = cells // n_t
+    while len(parts) > 1:
+        of = of * 2
+        parts = [
+            jnp.concatenate(merged(parts[i], parts[i + 1], of), axis=0) for i in range(0, len(parts), 2)
+        ]
+    channel_mean, square = parts[0][0:1], parts[0][1:2]
     channel_mean = jnp.broadcast_to(channel_mean, (8, c_n))
     size = c_n // GROUPS
     mean = group_sum(channel_mean) * (1.0 / size)
@@ -280,7 +307,7 @@
         ref[share:] = packed(table)
 
 
-def first_sum_body(n_h, n_dp, keep_ref, table_ref, *rest):
+def first_sum_body(n_h, keep_ref, table_ref, *rest):
     got, (own_ref, out_table), sends = rest[: n_h - 1], rest[n_h - 1 : n_h + 1], rest[n_h + 1 : -1]
     total = rest[-1]
     share, piece = keep_ref.shape[0], own_ref.shape[0]
@@ -345,6 +372,16 @@
             pl.when((h ^ s) == q)(put)
 
 
+def place_body(mask, own_ref, *rest):
+    out_hbm, wide, sem = rest[-3:]
+    share = own_ref.shape[0]
+    wide[...] = own_ref[...].astype(F32)
+    at = (lax.axis_index("height") ^ mask) * share
+    copy = pltpu.make_async_copy(wide, out_hbm.at[pl.ds(pl.multiple_of(at, 8), share)], sem)
+    copy.start()
+    copy.wait()
+
+
 def forward_body(
     n_edge, n_h,
     lat_ref, past_ref, norm_ref, kernel_ref, gain_ref, shift_ref, offset_ref, after_ref, *rest,
@@ -412,13 +449,14 @@
             out_ref[t, 2 * r + 1] = both
 
 
-def last_body(cells, dpre_ref, lat_ref, norm_ref, table_ref, gain_ref, out_ref, bias_ref, gains_ref, shifts_ref):
-    t_n, r_n, w_n, c_n = lat_ref.shape
+def last_body(cells, dpre_ref, lat_ref, norm_ref, table_ref, gain_ref, out_ref, bias_ref, gains_ref, shifts_ref, token_ref):
+    t_n, r_n, _, c_n = lat_ref.shape
     table, gain = table_ref[...], gain_ref[...]
     mean, rstd = norm_ref[0:1], norm_ref[1:2]
     scale = 1.0 / (cells * (c_n // GROUPS))
     means = group_sum(table * gain) * scale
     mean_b, mean_a = means[1:2], means[2:3]
+    token_ref[...] = jnp.zeros_like(token_ref)
     bias_ref[...] = table[0:1]
     gains_ref[...] = table[3:4]
     shifts_ref[...] = table[4:5]
@@ -442,48 +480,50 @@
     total = -(-rows // unit) * unit
     share, piece = total // n_h, total // (n_h * n_dp)
 
-    grad, bias_part, *corners = call(
-        functools.partial(fold_body, n_edge),
-        [shape(grid, BF16), small] + [shape(edge, BF16)] * n_edge,
-        cot,
-        scratch=[pltpu.VMEM((2, 2 * w_n, c_n), F32)],
-    )
+    lat, grad, bias_part, stats, *edge_list = call(
+        functools.partial(front_body, n_edge),
+        [shape(grid, BF16), shape(grid, BF16), small, small]
+        + [shape((2 * t_n * w_n + TAB, c_n), BF16)] * n_edge
+        + [shape(edge, BF16)] * n_edge,
+        pltpu.with_memory_space_constraint(cot, pltpu.HBM), pltpu.with_memory_space_constraint(lat, pltpu.HBM),
+        scratch=[
+            pltpu.VMEM(cot.shape, BF16),
+            pltpu.VMEM((2, 2 * w_n, c_n), F32),
+            pltpu.SemaphoreType.DMA((t_n * r_n,)),
+            pltpu.SemaphoreType.DMA((t_n,)),
+        ],
+        far=(0, 1),
+    )
+    edge_list, corners = edge_list[:n_edge], edge_list[n_edge:]
     halo = moved(grad, 1, 0)
+    edge_rows = facing(edge_list, 0)
     corner_rows = facing(corners, 1)
-    stats, *edge_list = call(
-        functools.partial(stats_body, n_edge),
-        [small] + [shape((2 * t_n * w_n + TAB, c_n), BF16)] * n_edge,
-        lat, grad,
-    )
-    edge_rows = facing(edge_list, 0)
-
-    rounds = [("height", 1 << i) for i in range(n_h.bit_length() - 1)]
-    rounds += [("tm", 1 << i) for i in range(n_t.bit_length() - 1)]
+
     cells = t_n * r_n * w_n
-    other = None
-    for axis, distance in rounds:
-        if other is not None:
-            (stats,) = call(functools.partial(merge_body, cells), [small], stats, other)
-        if n_h == 2 and axis == "height":
-            other = edge_rows[0]
-        else:
-            other = swap(stats, axis, distance)
+    for i in range(n_h.bit_length() - 1):
+        other = edge_rows[0] if n_h == 2 else swap(stats, "height", 1 << i)
         cells = cells * 2
-
-    fold, dact, lead = call(
+        (stats,) = call(functools.partial(merge_body, cells), [small], stats, other)
+    cells = cells * n_t
+    all_stats = [stats]
+    for s in range(1, n_t):
+        all_stats.append(swap(stats, "tm", s))
+    (lead,) = call(lead_body, [shape((t_n, r_n + n_edge, w_n, c_n), BF16)], lat, *edge_rows)
+    past = moved(lead, -1, 0)
+
+    fold, dact = call(
         functools.partial(back_body, n_edge, n_h),
-        [shape((t_n * r_n * w_n, 9 * c_n), BF16), shape(grid, F32), shape((t_n, r_n + n_edge, w_n, c_n), BF16)],
-        lat, stats, grad, halo, kernel, *edge_rows, *corner_rows,
+        [shape((t_n * r_n * w_n, 9 * c_n), BF16), shape(grid, F32)],
+        grad, halo, kernel, *edge_rows, *corner_rows,
         scratch=[pltpu.VMEM((3 * c_n, 9 * c_n), BF16)],
         room=6 << 20,
         flops=2 * 27 * t_n * r_n * w_n * c_n * c_n,
     )
-    past = moved(lead, -1, 0)
     keep, table, dpre, norm, *sends = call(
-        functools.partial(main_body, cells, n_h),
+        functools.partial(main_body, cells, n_h, n_t),
         [shape((share, c_n), F32), small, shape(grid, F32), small]
         + [shape((share + TAB, c_n), BF16)] * (n_h - 1),
-        lat, stats, other, fold, dact, gain, shift, bias_part,
+        lat, fold, dact, gain, shift, bias_part, *all_stats,
         scratch=[
             pltpu.VMEM((t_n * r_n * w_n, 3 * c_n), BF16),
             pltpu.VMEM((total, c_n), F32),
@@ -494,7 +534,7 @@
 
     got = [swap(send, "height", s) for s, send in enumerate(sends, 1)]
     own, table, *sends = call(
-        functools.partial(first_sum_body, n_h, n_dp),
+        functools.partial(first_sum_body, n_h),
         [shape((piece, c_n), F32), small] + [shape((piece + TAB, c_n), BF16)] * (n_dp - 1),
         keep, table, *got,
         scratch=[pltpu.VMEM((share, c_n), F32)],
@@ -522,14 +562,24 @@
             (part,) = call(pair_sum_body, [shape((piece + TAB, c_n), BF16)], part, other)
     part, table = call(last_sum_body, [shape((piece, c_n), BF16), small], part, other)
     got = [swap(part, "dp", s) for s in range(1, n_dp)]
-    latent_gradient, bias_grad, gain_grad, shift_grad = call(
+    latent_gradient, bias_grad, gain_grad, shift_grad, token = call(
         functools.partial(last_body, cells),
-        [shape(grid, BF16)] + [shape((1, c_n), F32)] * 3,
+        [shape(grid, BF16)] + [shape((1, c_n), F32)] * 3 + [small],
         dpre, lat, norm, table, gain,
     )
-    (half,) = call(gather_body, [shape((share, c_n), BF16)], shift_grad, part, *got)
+    (half,) = call(gather_body, [shape((share, c_n), BF16)], token, part, *got)
     got = [swap(half, "height", s) for s in range(1, n_h)]
-    (kernel_grad,) = call(spread_body, [shape((rows, c_n), F32)], half, *got)
+    if n_h == 2 and total == rows:
+        scratch = [pltpu.VMEM((share, c_n), F32), pltpu.SemaphoreType.DMA(())]
+        (kernel_grad,) = call(
+            functools.partial(place_body, 0), [shape((rows, c_n), F32)], half, scratch=scratch, far_out=(0,)
+        )
+        (kernel_grad,) = call(
+            functools.partial(place_body, 1), [shape((rows, c_n), F32)], *got, kernel_grad,
+            scratch=scratch, far=(1,), far_out=(0,), alias={1: 0},
+        )
+    else:
+        (kernel_grad,) = call(spread_body, [shape((rows, c_n), F32)], half, *got)
     return (
         upsampled[None],
         latent_gradient[None],

time: 65.9 us -> 61.3 us (0.930)
  waiting for transfers between devices: 24.5 us -> 19.8 us
  local copies, waits for them, and re-layouts: 3.01 us -> 0.02 us
  Pallas kernels: 11.7 us -> 13.7 us
  starting transfers between devices: 25.6 us -> 26.8 us
    ppermute x12 -> x13, waiting for transfers between devices: 19.1 us -> 11.8 us  [swap(): return lax.ppermute(block, axis, [(i, i ^ distance) for i in range(count)])]
    unnamed x16 -> x8, local copies, waits for them, and re-layouts: 3.01 us -> 0.02 us
    ppermute x2, waiting for transfers between devices: 0.01 us -> 2.9 us  [across(): return lax.ppermute(block, ('tm', 'height'), route)]
    pallas_call x14, Pallas kernels: 11.7 us -> 13.7 us  [call(): pl.pallas_call(body, out_shape=tuple(outs), in_specs=[HBM if i in far els...]
    ppermute x2, starting transfers between devices: 2.75 us -> 4.7 us  [moved(): return lax.ppermute(block, ('tm', 'height'), route)]
    ppermute x12 -> x13, starting transfers between devices: 21 us -> 20.2 us  [swap(): return lax.ppermute(block, axis, [(i, i ^ distance) for i in range(count)])]
  transfers between devices with their start and end apart: 16 -> 17, of which waited for: 9 -> 10; matrix products, arithmetic and copies ran while one was open for 0% -> 0% of each run, Pallas kernels for 11% -> 13%
where the time goes in v3:
time: 61.3 us; the launch traced here: 61.1 us
  starting transfers between devices  26.8 us (44%)
  waiting for transfers between devices  19.8 us (32%)
  Pallas kernels  13.7 us (22%)
  between operations  0.8 us (1%)
    ppermute x13, starting transfers between devices, swap(): return lax.ppermute(block, axis, [(i, i ^ distance) for i in range(count)])  20.2 us
    pallas_call x14, Pallas kernels, call(): pl.pallas_call(body, out_shape=tuple(outs), in_specs=[HBM if i in far els...  13.7 us
    ppermute x13, waiting for transfers between devices, swap(): return lax.ppermute(block, axis, [(i, i ^ distance) for i in range(count)])  11.8 us
    ppermute x2, waiting for transfers between devices, moved(): return lax.ppermute(block, ('tm', 'height'), route)  5.13 us
    ppermute x2, starting transfers between devices, moved(): return lax.ppermute(block, ('tm', 'height'), route)  4.7 us
    ppermute x2, waiting for transfers between devices, across(): return lax.ppermute(block, ('tm', 'height'), route)  2.9 us
    ppermute x2, starting transfers between devices, across(): return lax.ppermute(block, ('tm', 'height'), route)  1.84 us
  transfers between devices with their start and end apart: 17, of which 10 were waited for; matrix products, arithmetic and copies ran while one was open for 0% of the time, Pallas kernels for 13%

profile of v3, /device:TPU:0, one launch (start us, length us, event | category | flops | bytes accessed | tf_op | source)
XLA Modules:
  0.0 61.1 jit_solution(2567243700462632137)
XLA Ops:
  0.6 0.0 copy-start.1
  0.6 1.8 %shard_map.109 = (bf16[2,4,160,128]{3,2,1,0:T(8,128)(2,1)S(1)}, bf16[2,4,160,128]{3,2,1,0:T(8,128)(2,1)S(1)}, f32[8,128]{1,0:T(8,128)S(1)}, f32[8,128]{1,0:T(8,1...) custom-call(bf16[2,8,320,128]{3,2,1,0:T(8,128)(2,1)} %bitcast.18, bf16[2,4,160,128]{3,2,1,0:T(8,128)(2,1)} %bitcast.19), custom_call_target="tpu_custom_call" | custom-call | flops 1000000 | bytes 2555904 | tf_op jit(solution)/shard_map/pallas_call | solution.py:27
  2.5 1.3 %collective-permute-start.2 = (bf16[2,4,160,128]{3,2,1,0:T(8,128)(2,1)S(1)}, bf16[2,4,160,128]{3,2,1,0:T(8,128)(2,1)S(1)}, u32[]{:S(2)}, u32[]{:S(2)}) collective-permute-start(bf16[2,4,160,128]{3,2,1,0:T(8,128)(2,1)S(1)} %get-tuple-element.35.grad_ref), channel_id=1, source_target_pairs={{2,0},{3,1},{4,2},{5,3},{6,4},{7,5},{10,8},{11,9},{12,10},{13,11},... | collective-permute-start | bytes 983048 | tf_op jit(solution)/shard_map/ppermute | solution.py:55
  3.8 0.6 collective-permute-start
  4.4 1.3 %collective-permute-start.3 = (bf16[2,160,128]{2,1,0:T(8,128)(2,1)S(1)}, bf16[2,160,128]{2,1,0:T(8,128)(2,1)S(1)}, u32[]{:S(2)}, u32[]{:S(2)}) collective-permute-start(bf16[2,160,128]{2,1,0:T(8,128)(2,1)S(1)} %get-tuple-element.36), channel_id=1, source_target_pairs={{3,0},{2,1},{5,2},{4,3},{7,4},{6,5},{11,8},{10,9},{13,10},{12,11},... | collective-permute-start | bytes 245768 | tf_op jit(solution)/shard_map/ppermute | solution.py:65
  5.6 0.0 collective-permute-done.rest_0_.b_ref
  5.7 0.0 copy-start
  5.7 0.0 copy-start.2
  5.7 3.9 %collective-permute-start.4 = (f32[8,128]{1,0:T(8,128)S(1)}, f32[8,128]{1,0:T(8,128)S(1)}, u32[]{:S(2)}, u32[]{:S(2)}) collective-permute-start(f32[8,128]{1,0:T(8,128)S(1)} %shard_map.112.rest_0_), channel_id=1, source_target_pairs={{0,2},{2,0},{4,6},{6,4},{1,3},{3,1},{5,7},{7,5},{8,10},{10,8},{12,... | collective-permute-start | bytes 12296 | tf_op jit(solution)/shard_map/ppermute | solution.py:45
  9.6 3.6 %collective-permute-start.5 = (f32[8,128]{1,0:T(8,128)S(1)}, f32[8,128]{1,0:T(8,128)S(1)}, u32[]{:S(2)}, u32[]{:S(2)}) collective-permute-start(f32[8,128]{1,0:T(8,128)S(1)} %shard_map.112.rest_0_), channel_id=1, source_target_pairs={{0,4},{2,6},{4,0},{6,2},{1,5},{3,7},{5,1},{7,3},{8,12},{10,14},{12... | collective-permute-start | bytes 12296 | tf_op jit(solution)/shard_map/ppermute | solution.py:45
  13.2 0.0 collective-permute-start.6
  13.2 2.9 %collective-permute-done.3.rest_1_ = bf16[2,160,128]{2,1,0:T(8,128)(2,1)S(1)} collective-permute-done((bf16[2,160,128]{2,1,0:T(8,128)(2,1)S(1)}, bf16[2,160,128]{2,1,0:T(8,128)(2,1)S(1)}, u32[]{:S(2)}, u32[]{:S(2)}) %collective-permute-start.3) | collective-permute-done | bytes 81952 | tf_op jit(solution)/shard_map/ppermute | solution.py:65
  16.1 0.0 collective-permute-done.2.halo_ref
  16.1 2.1 %shard_map.111 = (bf16[1280,1152]{1,0:T(8,128)(2,1)S(1)}, f32[2,4,160,128]{3,2,1,0:T(8,128)S(1)}) custom-call(bf16[2,4,160,128]{3,2,1,0:T(8,128)(2,1)S(1)} %get-tuple-element.35.grad_ref, bf16[2,4,160,128]{3,2,1,0:T(8,128)(2,1)S(1)} %collective-permute-done.2.halo_ref, bf16[3,3,384,128]{3,2,1,0:T(8,128)(2,1)S(1)} %copy-done.1, ...), custom_call_target="tpu_custom_call" | custom-call | flops 1132462080 | bytes 5398528 | tf_op jit(solution)/shard_map/pallas_call | solution.py:27
  18.1 0.0 collective-permute-done.4.rest_1_
  18.2 0.1 collective-permute-done.5.rest_2_
  18.3 1.1 %collective-permute-done.6.rest_3_ = f32[8,128]{1,0:T(8,128)S(1)} collective-permute-done((f32[8,128]{1,0:T(8,128)S(1)}, f32[8,128]{1,0:T(8,128)S(1)}, u32[]{:S(2)}, u32[]{:S(2)}) %collective-permute-start.6) | collective-permute-done | bytes 4128 | tf_op jit(solution)/shard_map/ppermute | solution.py:45
  19.4 0.0 copy-done.2
  19.4 2.7 %shard_map.113 = (f32[1728,128]{1,0:T(8,128)S(1)}, f32[8,128]{1,0:T(8,128)S(1)}, f32[2,4,160,128]{3,2,1,0:T(8,128)S(1)}, f32[8,128]{1,0:T(8,128)S(1)}, bf16[1760,128]{1,0:T(8,128)(2,1)S(1)}) custom-call(bf16[2,4,160,128]{3,2,1,0:T(8,128)(2,1)S(1)} %get-tuple-element.33.lat_ref, bf16[1280,1152]{1,0:T(8,128)(2,1)S(1)} %get-tuple-element.37.fold_ref, ...), custom_call_target="tpu_custom_call" | custom-call | flops 1132462080 | bytes 5952512 | tf_op jit(solution)/shard_map/pallas_call | solution.py:27
  22.1 0.0 copy-start.3
  22.1 0.1 collective-permute-start.7
  22.2 3.4 %collective-permute-start.1 = (bf16[2,5,160,128]{3,2,1,0:T(8,128)(2,1)S(1)}, bf16[2,5,160,128]{3,2,1,0:T(8,128)(2,1)S(1)}, u32[]{:S(2)}, u32[]{:S(2)}) collective-permute-start(bf16[2,5,160,128]{3,2,1,0:T(8,128)(2,1)S(1)} %shard_map.110), channel_id=1, source_target_pairs={{0,2},{1,3},{2,4},{3,5},{4,6},{5,7},{8,10},{9,11},{10,12},{11,13},... | collective-permute-start | bytes 1228808 | tf_op jit(solution)/shard_map/ppermute | solution.py:55
  25.6 0.0 collective-permute-done.7.rest_0_
  25.6 0.2 shard_map.114
  25.8 2.5 %collective-permute-start.10 = (bf16[464,128]{1,0:T(8,128)(2,1)S(1)}, bf16[464,128]{1,0:T(8,128)(2,1)S(1)}, u32[]{:S(2)}, u32[]{:S(2)}) collective-permute-start(bf16[464,128]{1,0:T(8,128)(2,1)S(1)} %get-tuple-element.52), channel_id=1, source_target_pairs={{0,24},{8,16},{16,8},{24,0},{1,25},{9,17},{17,9},{25,1},{2,26},{10... | collective-permute-start | bytes 356360 | tf_op jit(solution)/shard_map/ppermute | solution.py:45
  28.3 0.5 collective-permute-start.8
  28.8 0.5 collective-permute-start.9
  29.4 5.1 %collective-permute-done.1.past_ref = bf16[2,5,160,128]{3,2,1,0:T(8,128)(2,1)S(1)} collective-permute-done((bf16[2,5,160,128]{3,2,1,0:T(8,128)(2,1)S(1)}, bf16[2,5,160,128]{3,2,1,0:T(8,128)(2,1)S(1)}, u32[]{:S(2)}, u32[]{:S(2)}) %collective-permute-start.1) | collective-permute-done | bytes 409632 | tf_op jit(solution)/shard_map/ppermute | solution.py:55
  34.5 3.7 %shard_map.115 = (bf16[2,8,320,128]{3,2,1,0:T(8,128)(2,1)}, f32[8,128]{1,0:T(8,128)S(1)}) custom-call(bf16[2,4,160,128]{3,2,1,0:T(8,128)(2,1)S(1)} %get-tuple-element.33.lat_ref, bf16[2,5,160,128]{3,2,1,0:T(8,128)(2,1)S(1)} %collective-permute-done.1.past_ref, f32[8,128]{1,0:T(8,128)S(1)} %get-tuple-element.41.norm_ref, ...), custom_call_target="tpu_custom_call" | custom-call | flops 1132462080 | bytes 3118592 | tf_op jit(solution)/shard_map/pallas_call | solution.py:27
  38.2 0.0 collective-permute-done.10.rest_2_
  38.2 0.0 collective-permute-done.8.rest_0_
  38.2 0.0 collective-permute-done.9.rest_1_
  38.2 0.1 shard_map.116.a_ref
  38.3 2.5 %collective-permute-start.11 = (bf16[464,128]{1,0:T(8,128)(2,1)S(1)}, bf16[464,128]{1,0:T(8,128)(2,1)S(1)}, u32[]{:S(2)}, u32[]{:S(2)}) collective-permute-start(bf16[464,128]{1,0:T(8,128)(2,1)S(1)} %shard_map.116.a_ref), channel_id=1, source_target_pairs={{0,2},{2,0},{4,6},{6,4},{1,3},{3,1},{5,7},{7,5},{8,10},{10,8},{12,... | collective-permute-start | bytes 356360 | tf_op jit(solution)/shard_map/ppermute | solution.py:45
  40.8 2.8 %collective-permute-done.11.b_ref = bf16[464,128]{1,0:T(8,128)(2,1)S(1)} collective-permute-done((bf16[464,128]{1,0:T(8,128)(2,1)S(1)}, bf16[464,128]{1,0:T(8,128)(2,1)S(1)}, u32[]{:S(2)}, u32[]{:S(2)}) %collective-permute-start.11) | collective-permute-done | bytes 118816 | tf_op jit(solution)/shard_map/ppermute | solution.py:45
  43.6 3.0 %collective-permute-start.12 = (bf16[464,128]{1,0:T(8,128)(2,1)S(1)}, bf16[464,128]{1,0:T(8,128)(2,1)S(1)}, u32[]{:S(2)}, u32[]{:S(2)}) collective-permute-start(bf16[464,128]{1,0:T(8,128)(2,1)S(1)} %shard_map.117.a_ref), channel_id=1, source_target_pairs={{0,4},{2,6},{4,0},{6,2},{1,5},{3,7},{5,1},{7,3},{8,12},{10,14},{12... | collective-permute-start | bytes 356360 | tf_op jit(solution)/shard_map/ppermute | solution.py:45
  46.7 2.8 %collective-permute-done.12.b_ref = bf16[464,128]{1,0:T(8,128)(2,1)S(1)} collective-permute-done((bf16[464,128]{1,0:T(8,128)(2,1)S(1)}, bf16[464,128]{1,0:T(8,128)(2,1)S(1)}, u32[]{:S(2)}, u32[]{:S(2)}) %collective-permute-start.12) | collective-permute-done | bytes 118816 | tf_op jit(solution)/shard_map/ppermute | solution.py:45
  49.5 1.6 %collective-permute-start.13 = (bf16[432,128]{1,0:T(8,128)(2,1)S(1)}, bf16[432,128]{1,0:T(8,128)(2,1)S(1)}, u32[]{:S(2)}, u32[]{:S(2)}) collective-permute-start(bf16[432,128]{1,0:T(8,128)(2,1)S(1)} %get-tuple-element.56.own_ref), channel_id=1, source_target_pairs={{0,8},{8,0},{16,24},{24,16},{1,9},{9,1},{17,25},{25,17},{2,10},{10... | collective-permute-start | bytes 331784 | tf_op jit(solution)/shard_map/ppermute | solution.py:45
  51.1 1.5 %collective-permute-start.14 = (bf16[432,128]{1,0:T(8,128)(2,1)S(1)}, bf16[432,128]{1,0:T(8,128)(2,1)S(1)}, u32[]{:S(2)}, u32[]{:S(2)}) collective-permute-start(bf16[432,128]{1,0:T(8,128)(2,1)S(1)} %get-tuple-element.56.own_ref), channel_id=1, source_target_pairs={{0,16},{8,24},{16,0},{24,8},{1,17},{9,25},{17,1},{25,9},{2,18},{10... | collective-permute-start | bytes 331784 | tf_op jit(solution)/shard_map/ppermute | solution.py:45
  52.6 0.5 collective-permute-start.15
  53.1 1.0 %shard_map.119 = (bf16[2,4,160,128]{3,2,1,0:T(8,128)(2,1)}, f32[1,128]{1,0:T(1,128)}, f32[1,128]{1,0:T(1,128)}, f32[1,128]{1,0:T(1,128)}, f32[8,128]{1,0:T(8,128)S(1)}) custom-call(f32[2,4,160,128]{3,2,1,0:T(8,128)S(1)} %get-tuple-element.47.dpre_ref, bf16[2,4,160,128]{3,2,1,0:T(8,128)(2,1)S(1)} %get-tuple-element.33.lat_ref, ...), custom_call_target="tpu_custom_call" | custom-call | flops 1000000 | bytes 1325056 | tf_op jit(solution)/shard_map/pallas_call | solution.py:27
  54.1 1.3 %collective-permute-done.13.rest_0_ = bf16[432,128]{1,0:T(8,128)(2,1)S(1)} collective-permute-done((bf16[432,128]{1,0:T(8,128)(2,1)S(1)}, bf16[432,128]{1,0:T(8,128)(2,1)S(1)}, u32[]{:S(2)}, u32[]{:S(2)}) %collective-permute-start.13) | collective-permute-done | bytes 110624 | tf_op jit(solution)/shard_map/ppermute | solution.py:45
  55.4 1.2 %collective-permute-done.14.rest_1_ = bf16[432,128]{1,0:T(8,128)(2,1)S(1)} collective-permute-done((bf16[432,128]{1,0:T(8,128)(2,1)S(1)}, bf16[432,128]{1,0:T(8,128)(2,1)S(1)}, u32[]{:S(2)}, u32[]{:S(2)}) %collective-permute-start.14) | collective-permute-done | bytes 110624 | tf_op jit(solution)/shard_map/ppermute | solution.py:45
  56.6 1.7 %collective-permute-done.15.rest_2_ = bf16[432,128]{1,0:T(8,128)(2,1)S(1)} collective-permute-done((bf16[432,128]{1,0:T(8,128)(2,1)S(1)}, bf16[432,128]{1,0:T(8,128)(2,1)S(1)}, u32[]{:S(2)}, u32[]{:S(2)}) %collective-permute-start.15) | collective-permute-done | bytes 110624 | tf_op jit(solution)/shard_map/ppermute | solution.py:45
  58.3 0.1 collective-permute-start.16
  58.4 1.0 %shard_map.121.rest_0_ = f32[3456,128]{1,0:T(8,128)} custom-call(bf16[1728,128]{1,0:T(8,128)(2,1)S(1)} %shard_map.120.own_ref), custom_call_target="tpu_custom_call" | custom-call | flops 1000000 | bytes 2211840 | tf_op jit(solution)/shard_map/pallas_call | solution.py:27
  59.3 0.8 %collective-permute-done.16.own_ref = bf16[1728,128]{1,0:T(8,128)(2,1)S(1)} collective-permute-done((bf16[1728,128]{1,0:T(8,128)(2,1)S(1)}, bf16[1728,128]{1,0:T(8,128)(2,1)S(1)}, u32[]{:S(2)}, u32[]{:S(2)}) %collective-permute-start.16) | collective-permute-done | bytes 442400 | tf_op jit(solution)/shard_map/ppermute | solution.py:45
  60.1 1.0 %shard_map.122 = f32[3456,128]{1,0:T(8,128)} custom-call(bf16[1728,128]{1,0:T(8,128)(2,1)S(1)} %collective-permute-done.16.own_ref, f32[3456,128]{1,0:T(8,128)} %shard_map.121.rest_0_), custom_call_target="tpu_custom_call", output_to_operand_aliasing={{}: (1, {})} | custom-call | flops 1000000 | bytes 3981312 | tf_op jit(solution)/shard_map/pallas_call | solution.py:27
  (8 shorter events, 0.2 us)
Async XLA Ops:
  0.6 15.4 %copy-start.1 = (bf16[3,3,384,128]{3,2,1,0:T(8,128)(2,1)S(1)}, bf16[3,3,384,128]{3,2,1,0:T(8,128)(2,1)}, u32[]{:S(2)}) copy-start(bf16[3,3,384,128]{3,2,1,0:T(8,128)(2,1)} %kernel_ref.3) | copy-start | bytes 2654212
  2.5 13.6 %collective-permute-start.2 = (bf16[2,4,160,128]{3,2,1,0:T(8,128)(2,1)S(1)}, bf16[2,4,160,128]{3,2,1,0:T(8,128)(2,1)S(1)}, u32[]{:S(2)}, u32[]{:S(2)}) collective-permute-start(bf16[2,4,160,128]{3,2,1,0:T(8,128)(2,1)S(1)} %get-tuple-element.35.grad_ref), channel_id=1, source_target_pairs={{2,0},{3,1},{4,2},{5,3},{6,4},{7,5},{10,8},{11,9},{12,10},{13,11},... | collective-permute-start | bytes 983048 | tf_op jit(solution)/shard_map/ppermute | solution.py:55
  3.8 1.8 %collective-permute-start = (bf16[672,128]{1,0:T(8,128)(2,1)S(1)}, bf16[672,128]{1,0:T(8,128)(2,1)S(1)}, u32[]{:S(2)}, u32[]{:S(2)}) collective-permute-start(bf16[672,128]{1,0:T(8,128)(2,1)S(1)} %get-tuple-element.34), channel_id=1, source_target_pairs={{1,0},{0,1},{3,2},{2,3},{5,4},{4,5},{7,6},{6,7},{9,8},{8,9},{11,10... | collective-permute-start | bytes 516104 | tf_op jit(solution)/shard_map/ppermute | solution.py:65
  4.4 11.7 %collective-permute-start.3 = (bf16[2,160,128]{2,1,0:T(8,128)(2,1)S(1)}, bf16[2,160,128]{2,1,0:T(8,128)(2,1)S(1)}, u32[]{:S(2)}, u32[]{:S(2)}) collective-permute-start(bf16[2,160,128]{2,1,0:T(8,128)(2,1)S(1)} %get-tuple-element.36), channel_id=1, source_target_pairs={{3,0},{2,1},{5,2},{4,3},{7,4},{6,5},{11,8},{10,9},{13,10},{12,11},... | collective-permute-start | bytes 245768 | tf_op jit(solution)/shard_map/ppermute | solution.py:65
  5.7 13.7 %copy-start = (f32[128]{0:T(128)S(1)}, f32[128]{0:T(128)}, u32[]{:S(2)}) copy-start(f32[128]{0:T(128)} %param.8) | copy-start | bytes 1540
  5.7 13.7 %copy-start.2 = (f32[128]{0:T(128)S(1)}, f32[128]{0:T(128)}, u32[]{:S(2)}) copy-start(f32[128]{0:T(128)} %param.9) | copy-start | bytes 1540
  5.7 12.4 %collective-permute-start.4 = (f32[8,128]{1,0:T(8,128)S(1)}, f32[8,128]{1,0:T(8,128)S(1)}, u32[]{:S(2)}, u32[]{:S(2)}) collective-permute-start(f32[8,128]{1,0:T(8,128)S(1)} %shard_map.112.rest_0_), channel_id=1, source_target_pairs={{0,2},{2,0},{4,6},{6,4},{1,3},{3,1},{5,7},{7,5},{8,10},{10,8},{12,... | collective-permute-start | bytes 12296 | tf_op jit(solution)/shard_map/ppermute | solution.py:45
  9.6 8.7 %collective-permute-start.5 = (f32[8,128]{1,0:T(8,128)S(1)}, f32[8,128]{1,0:T(8,128)S(1)}, u32[]{:S(2)}, u32[]{:S(2)}) collective-permute-start(f32[8,128]{1,0:T(8,128)S(1)} %shard_map.112.rest_0_), channel_id=1, source_target_pairs={{0,4},{2,6},{4,0},{6,2},{1,5},{3,7},{5,1},{7,3},{8,12},{10,14},{12... | collective-permute-start | bytes 12296 | tf_op jit(solution)/shard_map/ppermute | solution.py:45
  13.2 6.2 %collective-permute-start.6 = (f32[8,128]{1,0:T(8,128)S(1)}, f32[8,128]{1,0:T(8,128)S(1)}, u32[]{:S(2)}, u32[]{:S(2)}) collective-permute-start(f32[8,128]{1,0:T(8,128)S(1)} %shard_map.112.rest_0_), channel_id=1, source_target_pairs={{0,6},{2,4},{4,2},{6,0},{1,7},{3,5},{5,3},{7,1},{8,14},{10,12},{12... | collective-permute-start | bytes 12296 | tf_op jit(solution)/shard_map/ppermute | solution.py:45
  22.1 12.4 %copy-start.3 = (f32[128]{0:T(128)S(1)}, f32[128]{0:T(128)}, u32[]{:S(2)}) copy-start(f32[128]{0:T(128)} %param.11) | copy-start | bytes 1540
  22.1 3.5 %collective-permute-start.7 = (bf16[1760,128]{1,0:T(8,128)(2,1)S(1)}, bf16[1760,128]{1,0:T(8,128)(2,1)S(1)}, u32[]{:S(2)}, u32[]{:S(2)}) collective-permute-start(bf16[1760,128]{1,0:T(8,128)(2,1)S(1)} %get-tuple-element.44), channel_id=1, source_target_pairs={{0,1},{1,0},{2,3},{3,2},{4,5},{5,4},{6,7},{7,6},{8,9},{9,8},{10,11... | collective-permute-start | bytes 1351688 | tf_op jit(solution)/shard_map/ppermute | solution.py:45
  22.2 12.3 %collective-permute-start.1 = (bf16[2,5,160,128]{3,2,1,0:T(8,128)(2,1)S(1)}, bf16[2,5,160,128]{3,2,1,0:T(8,128)(2,1)S(1)}, u32[]{:S(2)}, u32[]{:S(2)}) collective-permute-start(bf16[2,5,160,128]{3,2,1,0:T(8,128)(2,1)S(1)} %shard_map.110), channel_id=1, source_target_pairs={{0,2},{1,3},{2,4},{3,5},{4,6},{5,7},{8,10},{9,11},{10,12},{11,13},... | collective-permute-start | bytes 1228808 | tf_op jit(solution)/shard_map/ppermute | solution.py:55
  25.8 12.4 %collective-permute-start.10 = (bf16[464,128]{1,0:T(8,128)(2,1)S(1)}, bf16[464,128]{1,0:T(8,128)(2,1)S(1)}, u32[]{:S(2)}, u32[]{:S(2)}) collective-permute-start(bf16[464,128]{1,0:T(8,128)(2,1)S(1)} %get-tuple-element.52), channel_id=1, source_target_pairs={{0,24},{8,16},{16,8},{24,0},{1,25},{9,17},{17,9},{25,1},{2,26},{10... | collective-permute-start | bytes 356360 | tf_op jit(solution)/shard_map/ppermute | solution.py:45
  28.3 9.9 %collective-permute-start.8 = (bf16[464,128]{1,0:T(8,128)(2,1)S(1)}, bf16[464,128]{1,0:T(8,128)(2,1)S(1)}, u32[]{:S(2)}, u32[]{:S(2)}) collective-permute-start(bf16[464,128]{1,0:T(8,128)(2,1)S(1)} %get-tuple-element.50), channel_id=1, source_target_pairs={{0,8},{8,0},{16,24},{24,16},{1,9},{9,1},{17,25},{25,17},{2,10},{10... | collective-permute-start | bytes 356360 | tf_op jit(solution)/shard_map/ppermute | solution.py:45
  28.8 9.3 %collective-permute-start.9 = (bf16[464,128]{1,0:T(8,128)(2,1)S(1)}, bf16[464,128]{1,0:T(8,128)(2,1)S(1)}, u32[]{:S(2)}, u32[]{:S(2)}) collective-permute-start(bf16[464,128]{1,0:T(8,128)(2,1)S(1)} %get-tuple-element.51), channel_id=1, source_target_pairs={{0,16},{8,24},{16,0},{24,8},{1,17},{9,25},{17,1},{25,9},{2,18},{10... | collective-permute-start | bytes 356360 | tf_op jit(solution)/shard_map/ppermute | solution.py:45
  38.3 5.3 %collective-permute-start.11 = (bf16[464,128]{1,0:T(8,128)(2,1)S(1)}, bf16[464,128]{1,0:T(8,128)(2,1)S(1)}, u32[]{:S(2)}, u32[]{:S(2)}) collective-permute-start(bf16[464,128]{1,0:T(8,128)(2,1)S(1)} %shard_map.116.a_ref), channel_id=1, source_target_pairs={{0,2},{2,0},{4,6},{6,4},{1,3},{3,1},{5,7},{7,5},{8,10},{10,8},{12,... | collective-permute-start | bytes 356360 | tf_op jit(solution)/shard_map/ppermute | solution.py:45
  43.6 5.9 %collective-permute-start.12 = (bf16[464,128]{1,0:T(8,128)(2,1)S(1)}, bf16[464,128]{1,0:T(8,128)(2,1)S(1)}, u32[]{:S(2)}, u32[]{:S(2)}) collective-permute-start(bf16[464,128]{1,0:T(8,128)(2,1)S(1)} %shard_map.117.a_ref), channel_id=1, source_target_pairs={{0,4},{2,6},{4,0},{6,2},{1,5},{3,7},{5,1},{7,3},{8,12},{10,14},{12... | collective-permute-start | bytes 356360 | tf_op jit(solution)/shard_map/ppermute | solution.py:45
  49.5 5.8 %collective-permute-start.13 = (bf16[432,128]{1,0:T(8,128)(2,1)S(1)}, bf16[432,128]{1,0:T(8,128)(2,1)S(1)}, u32[]{:S(2)}, u32[]{:S(2)}) collective-permute-start(bf16[432,128]{1,0:T(8,128)(2,1)S(1)} %get-tuple-element.56.own_ref), channel_id=1, source_target_pairs={{0,8},{8,0},{16,24},{24,16},{1,9},{9,1},{17,25},{25,17},{2,10},{10... | collective-permute-start | bytes 331784 | tf_op jit(solution)/shard_map/ppermute | solution.py:45
  51.1 5.5 %collective-permute-start.14 = (bf16[432,128]{1,0:T(8,128)(2,1)S(1)}, bf16[432,128]{1,0:T(8,128)(2,1)S(1)}, u32[]{:S(2)}, u32[]{:S(2)}) collective-permute-start(bf16[432,128]{1,0:T(8,128)(2,1)S(1)} %get-tuple-element.56.own_ref), channel_id=1, source_target_pairs={{0,16},{8,24},{16,0},{24,8},{1,17},{9,25},{17,1},{25,9},{2,18},{10... | collective-permute-start | bytes 331784 | tf_op jit(solution)/shard_map/ppermute | solution.py:45
  52.6 5.6 %collective-permute-start.15 = (bf16[432,128]{1,0:T(8,128)(2,1)S(1)}, bf16[432,128]{1,0:T(8,128)(2,1)S(1)}, u32[]{:S(2)}, u32[]{:S(2)}) collective-permute-start(bf16[432,128]{1,0:T(8,128)(2,1)S(1)} %get-tuple-element.56.own_ref), channel_id=1, source_target_pairs={{0,24},{8,16},{16,8},{24,0},{1,25},{9,17},{17,9},{25,1},{2,26},{10... | collective-permute-start | bytes 331784 | tf_op jit(solution)/shard_map/ppermute | solution.py:45
  58.3 1.9 %collective-permute-start.16 = (bf16[1728,128]{1,0:T(8,128)(2,1)S(1)}, bf16[1728,128]{1,0:T(8,128)(2,1)S(1)}, u32[]{:S(2)}, u32[]{:S(2)}) collective-permute-start(bf16[1728,128]{1,0:T(8,128)(2,1)S(1)} %shard_map.120.own_ref), channel_id=1, source_target_pairs={{0,1},{1,0},{2,3},{3,2},{4,5},{5,4},{6,7},{7,6},{8,9},{9,8},{10,11... | collective-permute-start | bytes 1327112 | tf_op jit(solution)/shard_map/ppermute | solution.py:45
